TPU v7x, 32 devices: a whole 2x2x4 slice. The times are simulated.
32 devices in a mesh: strip: 4 (over y, x), depth: 8 (over z, core).
Axes of the slice: x: 2, y: 2, z: 4, core: 2. Of those that a mesh axis runs over, the one named last changes fastest.
Arguments:
- volume: bfloat16 [64, 128, 2048], P('depth', 'strip'), may hold values from -6 to 6
- occupancy: int32 [8, 4, 16], P('depth', 'strip'), may hold values from 0 to 1
- slab_order: int32 [8], replicated, may hold values from 0 to 7, as said below
- w_in: bfloat16 [4, 64], replicated, may hold values from -3 to 3
- b_in: float32 [64], replicated, may hold values from -3 to 3
- w_out: bfloat16 [64, 4], replicated, may hold values from -1.5 to 1.5
- b_out: float32 [4], replicated, may hold values from -3 to 3
- conv_weight: float32 [3, 3, 3, 3], replicated, may hold values from -1.25 to 1.25
- conv_bias: float32 [3], replicated, may hold values from -3 to 3
Outputs:
- denoised: float32 [3, 4, 4, 8, 2048], P(None, 'strip', None, 'depth')
Inputs may be any that keep to these rules, and one draw needn't show every extreme that they name: slab_order is a permutation; for every bit b, bit b of slab_order[d] is bit b of d XOR a value that depends only on d's bits above b (so slabs that agree on their bits above b hold consecutive positions).
All inputs are finite; a program needn't handle non-finite values.
Results may differ from a plain program's by a relative error of at most 0.0003.
Values may be sent and summed in bfloat16 or wider, within the bound.
A program may use at most 64 MiB of HBM per device.

v0:
```python
import jax
import jax.numpy as jnp
from jax import lax
from jax.sharding import PartitionSpec as P

BRICK_ROWS = 32
BRICK_COLS = 128


def with_halo(cells, sides, width, closed):
    for axis, dim in sides:
        count = lax.axis_size(axis)
        ends = count if closed else count - 1
        head = lax.slice_in_dim(cells, 0, width, axis=dim)
        tail = lax.slice_in_dim(cells, cells.shape[dim] - width, cells.shape[dim], axis=dim)
        cells = jnp.concatenate(
            [
                lax.ppermute(tail, axis, [(i, (i + 1) % count) for i in range(ends)]),
                cells,
                lax.ppermute(head, axis, [((i + 1) % count, i) for i in range(ends)]),
            ],
            axis=dim,
        )
    return cells


def partner(block, axis, stride):
    count = lax.axis_size(axis)
    route = []
    for low in range(count):
        high = low | 1 << stride
        if high != low and high < count:
            route += [(low, high), (high, low)]
    return lax.ppermute(block, axis, route)


def expand_bricks(bricks):
    brick_rows_n, brick_cols_n = bricks.shape
    spread = jnp.broadcast_to(
        bricks.astype(jnp.float32)[:, None, :, None],
        (brick_rows_n, BRICK_ROWS, brick_cols_n, BRICK_COLS),
    )
    return spread.reshape(brick_rows_n * BRICK_ROWS, brick_cols_n * BRICK_COLS)


def march_slab(features, coverage, w_in, b_in, w_out, b_out, optical):
    rows_all = features.shape[2]
    cols_all = features.shape[3]

    def layer_step(state_pair, layer_feats):
        colour_sum, remaining = state_pair
        flattened = layer_feats.reshape(4, rows_all * cols_all)
        hidden = jax.nn.silu(
            jnp.dot(w_in.T, flattened, preferred_element_type=jnp.float32) + b_in[:, None]
        ).astype(jnp.bfloat16)
        output = jnp.dot(w_out.T, hidden, preferred_element_type=jnp.float32) + b_out[:, None]
        output = output.reshape(4, rows_all, cols_all)
        colour = jax.nn.sigmoid(output[:3])
        density = jax.nn.softplus(output[3]) * coverage
        alpha_val = 1.0 - jnp.exp(-optical * density)
        colour_sum = colour_sum + (remaining * alpha_val)[None] * colour
        remaining = remaining * (1.0 - alpha_val)
        return ((colour_sum, remaining), None)

    start = (
        jnp.zeros((3, rows_all, cols_all), jnp.float32),
        jnp.ones((rows_all, cols_all), jnp.float32),
    )
    (colour_sum, remaining), unused = lax.scan(layer_step, start, features)
    return (colour_sum, remaining)


def over_pair(front_part, back_part):
    colour = front_part[:3] + front_part[3:4] * back_part[:3]
    remaining = front_part[3:4] * back_part[3:4]
    return jnp.concatenate([colour, remaining], 0)


def shards(volume, occupancy, slab_order, w_in, b_in, w_out, b_out, conv_weight, conv_bias):
    depth_count = lax.axis_size("depth")
    depth_index = lax.axis_index("depth")
    strip_count = lax.axis_size("strip")
    strip_index = lax.axis_index("strip")
    layers, rows_here, columns = volume.shape
    optical = 2.0 / (layers * depth_count)
    rimmed = with_halo(volume, (("strip", 1),), 1, False).astype(jnp.float32)
    scalar_field = rimmed[:, 1:-1]
    grad_rows = 0.5 * (rimmed[:, 2:] - rimmed[:, :-2])
    padded_cols = jnp.pad(scalar_field, ((0, 0), (0, 0), (1, 1)))
    grad_cols = 0.5 * (padded_cols[:, :, 2:] - padded_cols[:, :, :-2])
    padded_depth = jnp.concatenate([scalar_field[:1], scalar_field, scalar_field[-1:]], 0)
    grad_depth = 0.5 * (padded_depth[2:] - padded_depth[:-2])
    features = jnp.stack([scalar_field, grad_cols, grad_rows, grad_depth], 1).astype(jnp.bfloat16)
    coverage = expand_bricks(occupancy[0])
    colour_sum, remaining = march_slab(features, coverage, w_in, b_in, w_out, b_out, optical)
    partial_value = jnp.concatenate([colour_sum, remaining[None]], 0)
    own_order = slab_order[depth_index]
    rounds = depth_count.bit_length() - 1
    row_share = rows_here // depth_count
    composed = partial_value
    for bit_index in range(rounds):
        pieces = composed.shape[1]
        paired = composed.reshape(4, pieces // 2, 2, columns)
        mine_bit = jnp.bitwise_and(jnp.right_shift(depth_index, bit_index), 1)
        keep_part = jnp.where(mine_bit == 0, paired[:, :, 0], paired[:, :, 1])
        give_part = jnp.where(mine_bit == 0, paired[:, :, 1], paired[:, :, 0])
        received = partner(give_part, "depth", bit_index)
        in_front = jnp.bitwise_and(jnp.right_shift(own_order, bit_index), 1) == 0
        front_part = jnp.where(in_front, keep_part, received)
        back_part = jnp.where(in_front, received, keep_part)
        composed = over_pair(front_part, back_part)
    picture = composed[:3][:, :, None, :]
    extended = with_halo(picture, (("strip", 1), ("depth", 2)), 1, True)
    edge_weight = jnp.concatenate(
        [
            (strip_index > 0).astype(jnp.float32)[None],
            jnp.ones((row_share,), jnp.float32),
            (strip_index < strip_count - 1).astype(jnp.float32)[None],
        ],
        0,
    )
    extended = extended * edge_weight[None, :, None, None]
    row_centre = extended[:, 1 : row_share + 1, 1]
    row_above = jnp.where(
        depth_index == 0, extended[:, 0:row_share, 0], extended[:, 1 : row_share + 1, 0]
    )
    row_below = jnp.where(
        depth_index == depth_count - 1,
        extended[:, 2 : row_share + 2, 2],
        extended[:, 1 : row_share + 1, 2],
    )
    row_sets = [row_above, row_centre, row_below]
    filtered = jnp.broadcast_to(conv_bias[:, None, None], (3, row_share, columns))
    for row_off in range(3):
        padded = jnp.pad(row_sets[row_off], ((0, 0), (0, 0), (1, 1)))
        for col_off in range(3):
            window = padded[:, :, col_off : col_off + columns]
            filtered = filtered + jnp.sum(
                conv_weight[:, :, row_off, col_off][:, :, None, None] * window[None], axis=1
            )
    return filtered.reshape(3, 1, row_share, 1, columns)


def solution(mesh):
    placed = (
        P("depth", "strip", None),
        P("depth", "strip", None),
        P(),
        P(),
        P(),
        P(),
        P(),
        P(),
        P(),
    )
    return jax.shard_map(
        shards,
        mesh=mesh,
        in_specs=placed,
        out_specs=P(None, "strip", None, "depth", None),
        check_vma=False,
    )
```

profile of v0, /device:TPU:27, one launch (start us, length us, event | category | flops | bytes accessed | tf_op | source)
XLA Modules:
  0.0 150.0 jit_solution(11306225657923054776)
XLA Ops:
  0.0 1.1 fusion.35
  1.1 3.1 %collective-permute-start = (bf16[8,1,2048]{2,1,0:T(2,128)(2,1)S(1)}, bf16[8,1,2048]{2,1,0:T(2,128)(2,1)S(1)}, u32[]{:S(2)}, u32[]{:S(2)}) collective-permute-start(bf16[8,1,2048]{2,1,0:T(2,128)(2,1)S(1)} %get-tuple-element.129), channel_id=1, source_target_pairs={{0,8},{8,16},{16,24},{1,9},{9,17},{17,25},{2,10},{10,18},{18,26},{... | collective-permute-start | bytes 98312 | tf_op jit(solution)/shard_map/ppermute | solution.py:18
  4.3 2.2 %collective-permute-start.1 = (bf16[8,1,2048]{2,1,0:T(2,128)(2,1)S(1)}, bf16[8,1,2048]{2,1,0:T(2,128)(2,1)S(1)}, u32[]{:S(2)}, u32[]{:S(2)}) collective-permute-start(bf16[8,1,2048]{2,1,0:T(2,128)(2,1)S(1)} %get-tuple-element.130), channel_id=1, source_target_pairs={{8,0},{16,8},{24,16},{9,1},{17,9},{25,17},{10,2},{18,10},{26,18},{... | collective-permute-start | bytes 98312 | tf_op jit(solution)/shard_map/ppermute | solution.py:20
  7.2 3.0 %collective-permute-done.1 = bf16[8,1,2048]{2,1,0:T(2,128)(2,1)S(1)} collective-permute-done((bf16[8,1,2048]{2,1,0:T(2,128)(2,1)S(1)}, bf16[8,1,2048]{2,1,0:T(2,128)(2,1)S(1)}, u32[]{:S(2)}, u32[]{:S(2)}) %collective-permute-start.1) | collective-permute-done | bytes 32800 | tf_op jit(solution)/shard_map/ppermute | solution.py:20
  10.2 1.7 %maximum_convert_fusion = f32[8,34,2048]{2,1,0:T(8,128)S(1)} fusion(bf16[8,1,2048]{2,1,0:T(2,128)(2,1)S(1)} %collective-permute-done.1, bf16[8,32,2048]{2,1,0:T(8,128)(2,1)} %param.11, bf16[8,1,2048]{2,1,0:T(2,128)(2,1)S(1)} %collective-permute-done), kind=kLoop, calls=%fused_computation.36 | loop fusion | flops 3342336 | bytes 3342336 | tf_op jit(solution)/shard_map/convert_element_type | solution.py:86
  13.6 1.4 fusion.23
  15.0 2.4 %pad_maximum_fusion = bf16[8,4,32,2048]{3,2,1,0:T(8,128)(2,1)} fusion(bf16[8,1,32,2048]{3,2,1,0:T(8,128)(2,1)S(1)} %get-tuple-element.126, bf16[8,1,32,2048]{3,2,1,0:T(8,128)(2,1)S(1)} %get-tuple-element.121, bf16[8,1,32,2048]{3,2,1,0:T(8,128)(2,1)S(1)} %get-tuple-element.125, bf16[8,1,32,2048]{3,2,1,0:T(8,128)(2,1)S(1)} %convert_bitcast_fusion), kind=kLoop, calls=%fused_computation.22 | loop fusion | flops 6291456 | bytes 8388608 | tf_op jit(solution)/shard_map/stack | solution.py:93
  17.4 91.8 %while.13 = (s32[]{:T(128)}, f32[3,32,2048]{2,1,0:T(8,128)S(1)}, f32[32,2048]{1,0:T(8,128)S(1)}, bf16[8,4,32,2048]{3,2,1,0:T(8,128)(2,1)}, bf16[4,64]{1,0:T(4,12...) while((s32[]{:T(128)}, f32[3,32,2048]{2,1,0:T(8,128)S(1)}, ...), condition=%wide.region_1.2_spmd.clone, body=%wide.region_0.1_spmd.clone.sunk | while | flops 94568448 | bytes 9971084 | solution.py:69
  17.4 1.1 dynamic-slice_bitcast_fusion.2
  18.9 7.6 %fusion.51 = f32[4,65536]{1,0:T(4,128)S(1)} fusion(bf16[64,4]{0,1:T(4,128)(2,1)S(1)} %get-tuple-element.241, bf16[4,65536]{1,0:T(4,128)(2,1)S(1)} %bitcast.163, bf16[4,64]{1,0:T(4,128)(2,1)S(1)} %get-tuple-element.239, f32[64]{0:T(128)S(1)} %get-tuple-element.240, f32[4]{0:T(128)S(1)} %get-tuple-element.242), kind=kOutput, calls=%fused_computation.4.clone.1 | convolution fusion | flops 92536832 | bytes 1574160 | tf_op jit(solution)/shard_map/while/body/eval_jaxpr/dot_general | solution.py:56
  30.4 7.6 %fusion.51 = f32[4,65536]{1,0:T(4,128)S(1)} fusion(bf16[64,4]{0,1:T(4,128)(2,1)S(1)} %get-tuple-element.241, bf16[4,65536]{1,0:T(4,128)(2,1)S(1)} %bitcast.163, bf16[4,64]{1,0:T(4,128)(2,1)S(1)} %get-tuple-element.239, f32[64]{0:T(128)S(1)} %get-tuple-element.240, f32[4]{0:T(128)S(1)} %get-tuple-element.242), kind=kOutput, calls=%fused_computation.4.clone.1 | convolution fusion | flops 92536832 | bytes 1574160 | tf_op jit(solution)/shard_map/while/body/eval_jaxpr/dot_general | solution.py:56
  40.3 1.1 dynamic-slice_bitcast_fusion.2
  41.8 7.6 %fusion.51 = f32[4,65536]{1,0:T(4,128)S(1)} fusion(bf16[64,4]{0,1:T(4,128)(2,1)S(1)} %get-tuple-element.241, bf16[4,65536]{1,0:T(4,128)(2,1)S(1)} %bitcast.163, bf16[4,64]{1,0:T(4,128)(2,1)S(1)} %get-tuple-element.239, f32[64]{0:T(128)S(1)} %get-tuple-element.240, f32[4]{0:T(128)S(1)} %get-tuple-element.242), kind=kOutput, calls=%fused_computation.4.clone.1 | convolution fusion | flops 92536832 | bytes 1574160 | tf_op jit(solution)/shard_map/while/body/eval_jaxpr/dot_general | solution.py:56
  51.7 1.1 dynamic-slice_bitcast_fusion.2
  53.3 7.6 %fusion.51 = f32[4,65536]{1,0:T(4,128)S(1)} fusion(bf16[64,4]{0,1:T(4,128)(2,1)S(1)} %get-tuple-element.241, bf16[4,65536]{1,0:T(4,128)(2,1)S(1)} %bitcast.163, bf16[4,64]{1,0:T(4,128)(2,1)S(1)} %get-tuple-element.239, f32[64]{0:T(128)S(1)} %get-tuple-element.240, f32[4]{0:T(128)S(1)} %get-tuple-element.242), kind=kOutput, calls=%fused_computation.4.clone.1 | convolution fusion | flops 92536832 | bytes 1574160 | tf_op jit(solution)/shard_map/while/body/eval_jaxpr/dot_general | solution.py:56
  63.2 1.1 dynamic-slice_bitcast_fusion.2
  64.7 7.6 %fusion.51 = f32[4,65536]{1,0:T(4,128)S(1)} fusion(bf16[64,4]{0,1:T(4,128)(2,1)S(1)} %get-tuple-element.241, bf16[4,65536]{1,0:T(4,128)(2,1)S(1)} %bitcast.163, bf16[4,64]{1,0:T(4,128)(2,1)S(1)} %get-tuple-element.239, f32[64]{0:T(128)S(1)} %get-tuple-element.240, f32[4]{0:T(128)S(1)} %get-tuple-element.242), kind=kOutput, calls=%fused_computation.4.clone.1 | convolution fusion | flops 92536832 | bytes 1574160 | tf_op jit(solution)/shard_map/while/body/eval_jaxpr/dot_general | solution.py:56
  74.6 1.1 dynamic-slice_bitcast_fusion.2
  76.1 7.6 %fusion.51 = f32[4,65536]{1,0:T(4,128)S(1)} fusion(bf16[64,4]{0,1:T(4,128)(2,1)S(1)} %get-tuple-element.241, bf16[4,65536]{1,0:T(4,128)(2,1)S(1)} %bitcast.163, bf16[4,64]{1,0:T(4,128)(2,1)S(1)} %get-tuple-element.239, f32[64]{0:T(128)S(1)} %get-tuple-element.240, f32[4]{0:T(128)S(1)} %get-tuple-element.242), kind=kOutput, calls=%fused_computation.4.clone.1 | convolution fusion | flops 92536832 | bytes 1574160 | tf_op jit(solution)/shard_map/while/body/eval_jaxpr/dot_general | solution.py:56
  86.1 1.1 dynamic-slice_bitcast_fusion.2
  87.6 7.6 %fusion.51 = f32[4,65536]{1,0:T(4,128)S(1)} fusion(bf16[64,4]{0,1:T(4,128)(2,1)S(1)} %get-tuple-element.241, bf16[4,65536]{1,0:T(4,128)(2,1)S(1)} %bitcast.163, bf16[4,64]{1,0:T(4,128)(2,1)S(1)} %get-tuple-element.239, f32[64]{0:T(128)S(1)} %get-tuple-element.240, f32[4]{0:T(128)S(1)} %get-tuple-element.242), kind=kOutput, calls=%fused_computation.4.clone.1 | convolution fusion | flops 92536832 | bytes 1574160 | tf_op jit(solution)/shard_map/while/body/eval_jaxpr/dot_general | solution.py:56
  97.5 1.1 dynamic-slice_bitcast_fusion.2
  99.0 7.6 %fusion.51 = f32[4,65536]{1,0:T(4,128)S(1)} fusion(bf16[64,4]{0,1:T(4,128)(2,1)S(1)} %get-tuple-element.241, bf16[4,65536]{1,0:T(4,128)(2,1)S(1)} %bitcast.163, bf16[4,64]{1,0:T(4,128)(2,1)S(1)} %get-tuple-element.239, f32[64]{0:T(128)S(1)} %get-tuple-element.240, f32[4]{0:T(128)S(1)} %get-tuple-element.242), kind=kOutput, calls=%fused_computation.4.clone.1 | convolution fusion | flops 92536832 | bytes 1574160 | tf_op jit(solution)/shard_map/while/body/eval_jaxpr/dot_general | solution.py:56
  111.1 2.2 %collective-permute-start.2 = (f32[4,16,2048]{2,0,1:T(4,128)S(1)}, f32[4,16,2048]{2,0,1:T(4,128)S(1)}, u32[]{:S(2)}, u32[]{:S(2)}) collective-permute-start(f32[4,16,2048]{2,0,1:T(4,128)S(1)} %get-tuple-element.117), channel_id=1, source_target_pairs={{0,1},{1,0},{2,3},{3,2},{4,5},{5,4},{6,7},{7,6},{8,9},{9,8},{10,11... | collective-permute-start | bytes 1572872 | tf_op jit(solution)/shard_map/ppermute | solution.py:34
  117.0 6.7 %collective-permute-done.3 = f32[4,8,2048]{2,0,1:T(4,128)S(1)} collective-permute-done((f32[4,8,2048]{2,0,1:T(4,128)S(1)}, f32[4,8,2048]{2,0,1:T(4,128)S(1)}, u32[]{:S(2)}, u32[]{:S(2)}) %collective-permute-start.3) | collective-permute-done | bytes 262176 | tf_op jit(solution)/shard_map/ppermute | solution.py:34
  125.0 8.1 %collective-permute-done.4 = f32[4,4,2048]{2,0,1:T(4,128)S(1)} collective-permute-done((f32[4,4,2048]{2,0,1:T(4,128)S(1)}, f32[4,4,2048]{2,0,1:T(4,128)S(1)}, u32[]{:S(2)}, u32[]{:S(2)}) %collective-permute-start.4) | collective-permute-done | bytes 131104 | tf_op jit(solution)/shard_map/ppermute | solution.py:34
  133.7 1.1 collective-permute-start.6
  134.9 1.3 collective-permute-done.5
  136.2 1.2 collective-permute-done.6
  137.4 2.1 %collective-permute-start.7 = (f32[3,6,1,2048]{3,0,1,2:T(4,128)S(1)}, f32[3,6,1,2048]{3,0,1,2:T(4,128)S(1)}, u32[]{:S(2)}, u32[]{:S(2)}) collective-permute-start(f32[3,6,1,2048]{3,0,1,2:T(4,128)S(1)} %pad_maximum_fusion.6), channel_id=1, source_target_pairs={{0,1},{1,2},{2,3},{3,4},{4,5},{5,6},{6,7},{7,0},{8,9},{9,10},{10,1... | collective-permute-start | bytes 442376 | tf_op jit(solution)/shard_map/ppermute | solution.py:18
  140.0 2.2 %collective-permute-done.7 = f32[3,6,1,2048]{3,0,1,2:T(4,128)S(1)} collective-permute-done((f32[3,6,1,2048]{3,0,1,2:T(4,128)S(1)}, f32[3,6,1,2048]{3,0,1,2:T(4,128)S(1)}, u32[]{:S(2)}, u32[]{:S(2)}) %collective-permute-start.7) | collective-permute-done | bytes 147488 | tf_op jit(solution)/shard_map/ppermute | solution.py:18
  142.2 4.2 %collective-permute-done.8 = f32[3,6,1,2048]{3,0,1,2:T(4,128)S(1)} collective-permute-done((f32[3,6,1,2048]{3,0,1,2:T(4,128)S(1)}, f32[3,6,1,2048]{3,0,1,2:T(4,128)S(1)}, u32[]{:S(2)}, u32[]{:S(2)}) %collective-permute-start.8) | collective-permute-done | bytes 147488 | tf_op jit(solution)/shard_map/ppermute | solution.py:20
  (127 shorter events, 34.3 us)
Async XLA Ops:
  1.1 6.0 %collective-permute-start = (bf16[8,1,2048]{2,1,0:T(2,128)(2,1)S(1)}, bf16[8,1,2048]{2,1,0:T(2,128)(2,1)S(1)}, u32[]{:S(2)}, u32[]{:S(2)}) collective-permute-start(bf16[8,1,2048]{2,1,0:T(2,128)(2,1)S(1)} %get-tuple-element.129), channel_id=1, source_target_pairs={{0,8},{8,16},{16,24},{1,9},{9,17},{17,25},{2,10},{10,18},{18,26},{... | collective-permute-start | bytes 98312 | tf_op jit(solution)/shard_map/ppermute | solution.py:18
  4.3 5.9 %collective-permute-start.1 = (bf16[8,1,2048]{2,1,0:T(2,128)(2,1)S(1)}, bf16[8,1,2048]{2,1,0:T(2,128)(2,1)S(1)}, u32[]{:S(2)}, u32[]{:S(2)}) collective-permute-start(bf16[8,1,2048]{2,1,0:T(2,128)(2,1)S(1)} %get-tuple-element.130), channel_id=1, source_target_pairs={{8,0},{16,8},{24,16},{9,1},{17,9},{25,17},{10,2},{18,10},{26,18},{... | collective-permute-start | bytes 98312 | tf_op jit(solution)/shard_map/ppermute | solution.py:20
  12.3 1.2 copy-start
  14.9 2.4 %copy-start.3 = (bf16[4,64]{1,0:T(4,128)(2,1)S(1)}, bf16[4,64]{1,0:T(4,128)(2,1)}, u32[]{:S(2)}) copy-start(bf16[4,64]{1,0:T(4,128)(2,1)} %param.14) | copy-start | bytes 1540
  15.0 2.4 %copy-start.4 = (bf16[64,4]{0,1:T(4,128)(2,1)S(1)}, bf16[64,4]{0,1:T(4,128)(2,1)}, u32[]{:S(2)}) copy-start(bf16[64,4]{0,1:T(4,128)(2,1)} %param.16) | copy-start | bytes 1540
  15.0 2.4 %copy-start.5 = (f32[64]{0:T(128)S(1)}, f32[64]{0:T(128)}, u32[]{:S(2)}) copy-start(f32[64]{0:T(128)} %param.15) | copy-start | bytes 772
  15.0 2.4 %copy-start.6 = (f32[4]{0:T(128)S(1)}, f32[4]{0:T(128)}, u32[]{:S(2)}) copy-start(f32[4]{0:T(128)} %param.17) | copy-start | bytes 52
  109.7 3.7 %copy-start.7 = (s32[8]{0:T(128)S(1)}, s32[8]{0:T(128)}, u32[]{:S(2)}) copy-start(s32[8]{0:T(128)} %param.13) | copy-start | bytes 100
  111.1 3.7 %collective-permute-start.2 = (f32[4,16,2048]{2,0,1:T(4,128)S(1)}, f32[4,16,2048]{2,0,1:T(4,128)S(1)}, u32[]{:S(2)}, u32[]{:S(2)}) collective-permute-start(f32[4,16,2048]{2,0,1:T(4,128)S(1)} %get-tuple-element.117), channel_id=1, source_target_pairs={{0,1},{1,0},{2,3},{3,2},{4,5},{5,4},{6,7},{7,6},{8,9},{9,8},{10,11... | collective-permute-start | bytes 1572872 | tf_op jit(solution)/shard_map/ppermute | solution.py:34
  116.1 7.6 %collective-permute-start.3 = (f32[4,8,2048]{2,0,1:T(4,128)S(1)}, f32[4,8,2048]{2,0,1:T(4,128)S(1)}, u32[]{:S(2)}, u32[]{:S(2)}) collective-permute-start(f32[4,8,2048]{2,0,1:T(4,128)S(1)} %select_bitcast_fusion.1), channel_id=1, source_target_pairs={{0,2},{2,0},{1,3},{3,1},{4,6},{6,4},{5,7},{7,5},{8,10},{10,8},{9,1... | collective-permute-start | bytes 786440 | tf_op jit(solution)/shard_map/ppermute | solution.py:34
  123.7 16.1 %copy-start.1 = (f32[3,3,3,3]{3,2,1,0:T(4,128)S(1)}, f32[3,3,3,3]{3,2,1,0:T(4,128)}, u32[]{:S(2)}) copy-start(f32[3,3,3,3]{3,2,1,0:T(4,128)} %param.18) | copy-start | bytes 976
  124.2 8.9 %collective-permute-start.4 = (f32[4,4,2048]{2,0,1:T(4,128)S(1)}, f32[4,4,2048]{2,0,1:T(4,128)S(1)}, u32[]{:S(2)}, u32[]{:S(2)}) collective-permute-start(f32[4,4,2048]{2,0,1:T(4,128)S(1)} %select_bitcast_fusion.2), channel_id=1, source_target_pairs={{0,4},{4,0},{1,5},{5,1},{2,6},{6,2},{3,7},{7,3},{8,12},{12,8},{9,1... | collective-permute-start | bytes 393224 | tf_op jit(solution)/shard_map/ppermute | solution.py:34
  133.4 2.8 %collective-permute-start.5 = (f32[3,1,1,2048]{3,0,1,2:T(4,128)S(1)}, f32[3,1,1,2048]{3,0,1,2:T(4,128)S(1)}, u32[]{:S(2)}, u32[]{:S(2)}) collective-permute-start(f32[3,1,1,2048]{3,0,1,2:T(4,128)S(1)} %get-tuple-element.146), channel_id=1, source_target_pairs={{0,8},{8,16},{16,24},{24,0},{1,9},{9,17},{17,25},{25,1},{2,10},{10... | collective-permute-start | bytes 73736 | tf_op jit(solution)/shard_map/ppermute | solution.py:18
  133.7 3.7 %collective-permute-start.6 = (f32[3,1,1,2048]{3,0,1,2:T(4,128)S(1)}, f32[3,1,1,2048]{3,0,1,2:T(4,128)S(1)}, u32[]{:S(2)}, u32[]{:S(2)}) collective-permute-start(f32[3,1,1,2048]{3,0,1,2:T(4,128)S(1)} %get-tuple-element.147), channel_id=1, source_target_pairs={{8,0},{16,8},{24,16},{0,24},{9,1},{17,9},{25,17},{1,25},{10,2},{18... | collective-permute-start | bytes 73736 | tf_op jit(solution)/shard_map/ppermute | solution.py:20
  137.4 4.8 %collective-permute-start.7 = (f32[3,6,1,2048]{3,0,1,2:T(4,128)S(1)}, f32[3,6,1,2048]{3,0,1,2:T(4,128)S(1)}, u32[]{:S(2)}, u32[]{:S(2)}) collective-permute-start(f32[3,6,1,2048]{3,0,1,2:T(4,128)S(1)} %pad_maximum_fusion.6), channel_id=1, source_target_pairs={{0,1},{1,2},{2,3},{3,4},{4,5},{5,6},{6,7},{7,0},{8,9},{9,10},{10,1... | collective-permute-start | bytes 442376 | tf_op jit(solution)/shard_map/ppermute | solution.py:18
  139.5 6.9 %collective-permute-start.8 = (f32[3,6,1,2048]{3,0,1,2:T(4,128)S(1)}, f32[3,6,1,2048]{3,0,1,2:T(4,128)S(1)}, u32[]{:S(2)}, u32[]{:S(2)}) collective-permute-start(f32[3,6,1,2048]{3,0,1,2:T(4,128)S(1)} %pad_maximum_fusion.6), channel_id=1, source_target_pairs={{1,0},{2,1},{3,2},{4,3},{5,4},{6,5},{7,6},{0,7},{9,8},{10,9},{11,1... | collective-permute-start | bytes 442376 | tf_op jit(solution)/shard_map/ppermute | solution.py:20
  146.7 2.4 %copy-start.2 = (f32[3]{0:T(128)S(1)}, f32[3]{0:T(128)}, u32[]{:S(2)}) copy-start(f32[3]{0:T(128)} %param.19) | copy-start | bytes 40
where the time goes:
time: 152 us; the launch traced here: 150 us
  matrix products  61.1 us (40%)
  waiting for transfers between devices  27 us (18%)
  local copies, waits for them, and re-layouts  25.1 us (17%)
  other arithmetic  22.2 us (15%)
  starting transfers between devices  11.6 us (8%)
  between operations  2.39 us (2%)
    dot_general x8, matrix products, layer_step(): jnp.dot(w_out.T, hidden, preferred_element_type=jnp.float32)  61.1 us
    ppermute x3, waiting for transfers between devices, partner(): return lax.ppermute(block, axis, route)  15.1 us
    while x16, local copies, waits for them, and re-layouts  11.9 us
    ppermute x3, waiting for transfers between devices, with_halo(): lax.ppermute(head, axis, [((i + 1) % count, i) for i in range(ends)])  8.45 us
    slice x8, local copies, waits for them, and re-layouts, layer_step(): density = jax.nn.softplus(output[3]) * coverage  6.04 us
    ppermute x3, starting transfers between devices, with_halo(): lax.ppermute(tail, axis, [(i, (i + 1) % count) for i in range(ends)])  5.59 us
    add x8, other arithmetic, layer_step(): colour_sum = colour_sum + (remaining * alpha_val)[None] * colour  5.35 us
    div x8, other arithmetic, layer_step(): colour = jax.nn.sigmoid(output[:3])  4.4 us
  transfers between devices with their start and end apart: 9, of which 8 were waited for; matrix products, arithmetic and copies ran while one was open for 1% of the time, Pallas kernels for 0%

commit v1 on v0

--- a/solution.py
+++ b/solution.py
@@ -1,11 +1,12 @@
+import functools
+
 import jax
 import jax.numpy as jnp
+import numpy as np
 from jax import lax
+from jax.experimental import pallas as pl
+from jax.experimental.pallas import tpu as pltpu
 from jax.sharding import PartitionSpec as P
-
-BRICK_ROWS = 32
-BRICK_COLS = 128
-
 
 def with_halo(cells, sides, width, closed):
     for axis, dim in sides:
@@ -34,40 +35,134 @@
     return lax.ppermute(block, axis, route)
 
 
-def expand_bricks(bricks):
-    brick_rows_n, brick_cols_n = bricks.shape
-    spread = jnp.broadcast_to(
-        bricks.astype(jnp.float32)[:, None, :, None],
-        (brick_rows_n, BRICK_ROWS, brick_cols_n, BRICK_COLS),
-    )
-    return spread.reshape(brick_rows_n * BRICK_ROWS, brick_cols_n * BRICK_COLS)
-
-
-def march_slab(features, coverage, w_in, b_in, w_out, b_out, optical):
-    rows_all = features.shape[2]
-    cols_all = features.shape[3]
-
-    def layer_step(state_pair, layer_feats):
-        colour_sum, remaining = state_pair
-        flattened = layer_feats.reshape(4, rows_all * cols_all)
-        hidden = jax.nn.silu(
-            jnp.dot(w_in.T, flattened, preferred_element_type=jnp.float32) + b_in[:, None]
-        ).astype(jnp.bfloat16)
-        output = jnp.dot(w_out.T, hidden, preferred_element_type=jnp.float32) + b_out[:, None]
-        output = output.reshape(4, rows_all, cols_all)
-        colour = jax.nn.sigmoid(output[:3])
-        density = jax.nn.softplus(output[3]) * coverage
-        alpha_val = 1.0 - jnp.exp(-optical * density)
-        colour_sum = colour_sum + (remaining * alpha_val)[None] * colour
-        remaining = remaining * (1.0 - alpha_val)
-        return ((colour_sum, remaining), None)
-
-    start = (
-        jnp.zeros((3, rows_all, cols_all), jnp.float32),
-        jnp.ones((rows_all, cols_all), jnp.float32),
-    )
-    (colour_sum, remaining), unused = lax.scan(layer_step, start, features)
-    return (colour_sum, remaining)
+LANES = 128
+
+
+def march_kernel(optical, unroll, occ_ref, vol_ref, above_ref, below_ref, lhs_ref, mix_ref, bias_ref, out_ref, feat, picks):
+    layers, rows, cols = vol_ref.shape
+    bricks = occ_ref.shape[0]
+    tiles = out_ref.shape[0]
+    lane = lax.broadcasted_iota(jnp.int32, (rows, cols), 1)
+    row = lax.broadcasted_iota(jnp.int32, (rows, cols), 0)
+    first_col, last_col = lane == 0, lane == cols - 1
+    first_row, last_row = row == 0, row == rows - 1
+    ones = jnp.ones((feat.shape[1] - 4 * rows, cols), jnp.bfloat16)
+
+    def features(z, carry):
+        here = vol_ref[z].astype(jnp.float32)
+        right = jnp.where(last_col, 0.0, pltpu.roll(here, cols - 1, 1))
+        left = jnp.where(first_col, 0.0, pltpu.roll(here, 1, 1))
+        down = jnp.where(last_row, below_ref[z].astype(jnp.float32), pltpu.roll(here, rows - 1, 0))
+        up = jnp.where(first_row, above_ref[z].astype(jnp.float32), pltpu.roll(here, 1, 0))
+        far = vol_ref[jnp.minimum(z + 1, layers - 1)].astype(jnp.float32)
+        near = vol_ref[jnp.maximum(z - 1, 0)].astype(jnp.float32)
+        feat[z, 0:rows] = vol_ref[z]
+        feat[z, rows:2 * rows] = (0.5 * (right - left)).astype(jnp.bfloat16)
+        feat[z, 2 * rows:3 * rows] = (0.5 * (down - up)).astype(jnp.bfloat16)
+        feat[z, 3 * rows:4 * rows] = (0.5 * (far - near)).astype(jnp.bfloat16)
+        feat[z, 4 * rows:] = ones
+        return carry
+
+    lax.fori_loop(0, layers, features, 0)
+    out_ref[:, :3] = jnp.zeros((tiles, 3, 8, cols), jnp.float32)
+    out_ref[:, 3:] = jnp.ones((tiles, 1, 8, cols), jnp.float32)
+
+    def pick(i, found):
+        picks[found] = i
+        return found + (occ_ref[i] != 0).astype(jnp.int32)
+
+    found = lax.fori_loop(0, bricks, pick, 0)
+
+    def pair(step, carry):
+        part = step // tiles
+        tile = step % tiles
+        low = pl.ds(pl.multiple_of(picks[2 * part] * LANES, LANES), LANES)
+        high = pl.ds(pl.multiple_of(picks[jnp.minimum(2 * part + 1, found - 1)] * LANES, LANES), LANES)
+
+        def layer(z, state):
+            colour, remaining = state
+            x = jnp.concatenate([feat[z, :, low], feat[z, :, high]], 1)
+            out = bias_ref[...]
+            for p in range(2):
+                u = jnp.dot(lhs_ref[2 * tile + p], x, preferred_element_type=jnp.float32)
+                hidden = (u + u * jnp.tanh(u)).astype(jnp.bfloat16)
+                out = out + jnp.dot(mix_ref[p], hidden, preferred_element_type=jnp.float32)
+            raw = out[24:32]
+            density = jnp.maximum(raw, 0.0) + jnp.log1p(jnp.exp(-jnp.abs(raw)))
+            keep = jnp.exp(-optical * density)
+            weight = 0.5 * (remaining * (1.0 - keep))
+            colour = tuple(
+                colour[i] + (weight + weight * jnp.tanh(out[8 * i:8 * i + 8])) for i in range(3)
+            )
+            return colour, remaining * keep
+
+        zero = jnp.zeros((8, 2 * LANES), jnp.float32)
+        state = ((zero, zero, zero), jnp.ones((8, 2 * LANES), jnp.float32))
+
+        def layer_group(group, state):
+            for k in range(unroll):
+                state = layer(group * unroll + k, state)
+            return state
+
+        if unroll == layers:
+            state = layer_group(0, state)
+        else:
+            state = lax.fori_loop(0, layers // unroll, layer_group, state)
+        colour, remaining = state
+        for i, value in enumerate(colour + (remaining,)):
+            out_ref[tile, i, :, low] = value[:, :LANES]
+            out_ref[tile, i, :, high] = value[:, LANES:]
+        return carry
+
+    lax.fori_loop(0, (found + 1) // 2 * tiles, pair, 0)
+
+
+def march(volume, above, below, occupancy, w_in, b_in, w_out, b_out, depth_count, optical):
+    layers, rows, cols = volume.shape
+    channels, hidden = w_in.shape
+    tiles = rows // 8
+    share = rows // depth_count
+    pos_row = np.zeros((tiles, 8), np.int64)
+    for r in range(rows):
+        d, k = r % depth_count, r // depth_count
+        pos_row[d % tiles, d // tiles * share + k] = r
+    chosen = np.zeros((rows, rows), np.float32)
+    chosen[np.arange(rows), pos_row.reshape(-1)] = 1.0
+    half_in = 0.5 * w_in.astype(jnp.float32)
+    spread = jnp.asarray(chosen)[:, None, None, :] * half_in.T[None, :, :, None]
+    spread = spread.reshape(rows * hidden, channels * rows)
+    rest = 0.5 * b_in
+    parts = []
+    for unused in range(3):
+        part = lax.reduce_precision(rest, 8, 7)
+        parts.append(part)
+        rest = rest - part
+    parts = jnp.stack(parts + [jnp.zeros_like(b_in)] * 13, 1)
+    parts = jnp.broadcast_to(parts[None], (rows, hidden, 16)).reshape(rows * hidden, 16)
+    lhs = jnp.concatenate([spread, parts], 1).astype(jnp.bfloat16)
+    lhs = lhs.reshape(2 * tiles, 4 * hidden, channels * rows + 16)
+    scale = jnp.asarray(np.array([0.5, 0.5, 0.5, 1.0], np.float32))
+    place = np.zeros((2, 8, 4), np.float32)
+    for p in range(2):
+        for i in range(4):
+            place[p, 4 * p + i, i] = 1.0
+    scaled_out = w_out.astype(jnp.float32) * scale[None]
+    mix = scaled_out.T[None, :, None, None, :] * jnp.asarray(place)[:, None, :, :, None]
+    mix = mix.reshape(2, 32, 4 * hidden).astype(jnp.bfloat16)
+    bias = jnp.broadcast_to((b_out * scale)[:, None, None], (4, 8, 2 * LANES)).reshape(32, 2 * LANES)
+    vmem = pl.BlockSpec(memory_space=pltpu.VMEM)
+    return pl.pallas_call(
+        functools.partial(march_kernel, optical, 8),
+        out_shape=jax.ShapeDtypeStruct((tiles, 4, 8, cols), jnp.float32),
+        in_specs=[pl.BlockSpec(memory_space=pltpu.SMEM)] + [vmem] * 6,
+        out_specs=vmem,
+        scratch_shapes=[
+            pltpu.VMEM((layers, channels * rows + 16, cols), jnp.bfloat16),
+            pltpu.SMEM((occupancy.size + 1,), jnp.int32),
+        ],
+        compiler_params=pltpu.CompilerParams(vmem_limit_bytes=40 * 1024 * 1024),
+        name="march",
+    )(occupancy.reshape(-1), volume, above, below, lhs, mix, bias)
 
 
 def over_pair(front_part, back_part):
@@ -83,24 +178,23 @@
     strip_index = lax.axis_index("strip")
     layers, rows_here, columns = volume.shape
     optical = 2.0 / (layers * depth_count)
-    rimmed = with_halo(volume, (("strip", 1),), 1, False).astype(jnp.float32)
-    scalar_field = rimmed[:, 1:-1]
-    grad_rows = 0.5 * (rimmed[:, 2:] - rimmed[:, :-2])
-    padded_cols = jnp.pad(scalar_field, ((0, 0), (0, 0), (1, 1)))
-    grad_cols = 0.5 * (padded_cols[:, :, 2:] - padded_cols[:, :, :-2])
-    padded_depth = jnp.concatenate([scalar_field[:1], scalar_field, scalar_field[-1:]], 0)
-    grad_depth = 0.5 * (padded_depth[2:] - padded_depth[:-2])
-    features = jnp.stack([scalar_field, grad_cols, grad_rows, grad_depth], 1).astype(jnp.bfloat16)
-    coverage = expand_bricks(occupancy[0])
-    colour_sum, remaining = march_slab(features, coverage, w_in, b_in, w_out, b_out, optical)
-    partial_value = jnp.concatenate([colour_sum, remaining[None]], 0)
+    down_route = [(i, i + 1) for i in range(strip_count - 1)]
+    up_route = [(i + 1, i) for i in range(strip_count - 1)]
+    above = lax.ppermute(volume[:, rows_here - 1 :], "strip", down_route)
+    below = lax.ppermute(volume[:, :1], "strip", up_route)
+    partial_value = march(
+        volume, above, below, occupancy, w_in, b_in, w_out, b_out, depth_count, optical
+    )
     own_order = slab_order[depth_index]
     rounds = depth_count.bit_length() - 1
     row_share = rows_here // depth_count
-    composed = partial_value
+    tiles = partial_value.shape[0]
+    composed = partial_value.transpose(1, 0, 2, 3)
     for bit_index in range(rounds):
-        pieces = composed.shape[1]
-        paired = composed.reshape(4, pieces // 2, 2, columns)
+        if composed.shape[1] > 1:
+            paired = composed.reshape(4, composed.shape[1] // 2, 2, composed.shape[2], columns)
+        else:
+            paired = composed.reshape(4, composed.shape[2] // 2 // row_share, 2, row_share, columns)
         mine_bit = jnp.bitwise_and(jnp.right_shift(depth_index, bit_index), 1)
         keep_part = jnp.where(mine_bit == 0, paired[:, :, 0], paired[:, :, 1])
         give_part = jnp.where(mine_bit == 0, paired[:, :, 1], paired[:, :, 0])
@@ -109,6 +203,9 @@
         front_part = jnp.where(in_front, keep_part, received)
         back_part = jnp.where(in_front, received, keep_part)
         composed = over_pair(front_part, back_part)
+        if paired.shape[3] == row_share and tiles >> (bit_index + 1) < 1:
+            composed = composed.reshape(4, 1, -1, columns)
+    composed = composed.reshape(4, row_share, columns)
     picture = composed[:3][:, :, None, :]
     extended = with_halo(picture, (("strip", 1), ("depth", 2)), 1, True)
     edge_weight = jnp.concatenate(

time: 152 us -> 126 us (0.83)
  matrix products: 61.1 us -> 0 us
  Pallas kernels: 0 us -> 38.8 us
  starting transfers between devices: 11.6 us -> 50 us
  local copies, waits for them, and re-layouts: 25.1 us -> 6.52 us
  other arithmetic: 22.2 us -> 4.8 us
  waiting for transfers between devices: 27 us -> 22 us
    dot_general x8 -> x0, matrix products: 61.1 us -> none  [layer_step(): jnp.dot(w_out.T, hidden, preferred_element_type=jnp.float32)]
    pallas_call x0 -> x1, Pallas kernels: none -> 38.8 us  [march(): pl.pallas_call(functools.partial(march_kernel, optical, 8), out_shape=jax...]
    ppermute x3, starting transfers between devices: 2.53 us -> 38.3 us  [partner(): return lax.ppermute(block, axis, route)]
    while x16 -> x0, local copies, waits for them, and re-layouts: 11.9 us -> none
    add x8 -> x0, other arithmetic: 5.35 us -> none  [layer_step(): colour_sum = colour_sum + (remaining * alpha_val)[None] * colour]
    ppermute x0 -> x2, starting transfers between devices: none -> 5.28 us  [the longest x1 3.12 us: shards(): above = lax.ppermute(volume[:, rows_here - 1:], 'strip', down_route)]
    slice x9 -> x1, local copies, waits for them, and re-layouts: 6.07 us -> 1.13 us  [shards(): below = lax.ppermute(volume[:, :1], 'strip', up_route)]
    div x8 -> x0, other arithmetic: 4.4 us -> none  [layer_step(): colour = jax.nn.sigmoid(output[:3])]
  transfers between devices with their start and end apart: 9 -> 9, of which waited for: 8 -> 7; matrix products, arithmetic and copies ran while one was open for 1% -> 4% of each run, Pallas kernels for 0% -> 0%
where the time goes in v1:
time: 126 us; the launch traced here: 124 us
  starting transfers between devices  50 us (40%)
  Pallas kernels  38.8 us (31%)
  waiting for transfers between devices  22 us (17%)
  local copies, waits for them, and re-layouts  6.52 us (5%)
  other arithmetic  4.8 us (4%)
  between operations  2.34 us (2%)
    pallas_call x1, Pallas kernels, march(): pl.pallas_call(functools.partial(march_kernel, optical, 8), out_shape=jax...  38.8 us
    ppermute x3, starting transfers between devices, partner(): return lax.ppermute(block, axis, route)  38.3 us
    ppermute x3, waiting for transfers between devices, partner(): return lax.ppermute(block, axis, route)  11.9 us
    ppermute x2, starting transfers between devices, with_halo(): lax.ppermute(tail, axis, [(i, (i + 1) % count) for i in range(ends)])  6.41 us
    ppermute x2, waiting for transfers between devices, with_halo(): lax.ppermute(head, axis, [((i + 1) % count, i) for i in range(ends)])  5.12 us
    ppermute x2, waiting for transfers between devices, with_halo(): lax.ppermute(tail, axis, [(i, (i + 1) % count) for i in range(ends)])  4.97 us
    ppermute x1, starting transfers between devices, shards(): above = lax.ppermute(volume[:, rows_here - 1:], 'strip', down_route)  3.12 us
  transfers between devices with their start and end apart: 9, of which 7 were waited for; matrix products, arithmetic and copies ran while one was open for 4% of the time, Pallas kernels for 0%

profile of v1, /device:TPU:27, one launch (start us, length us, event | category | flops | bytes accessed | tf_op | source)
XLA Modules:
  0.0 124.4 jit_solution(837683192406656053)
XLA Ops:
  0.0 1.1 fusion.10
  1.1 3.1 %collective-permute-start = (bf16[8,1,2048]{2,1,0:T(2,128)(2,1)S(1)}, bf16[8,1,2048]{2,1,0:T(2,128)(2,1)S(1)}, u32[]{:S(2)}, u32[]{:S(2)}) collective-permute-start(bf16[8,1,2048]{2,1,0:T(2,128)(2,1)S(1)} %get-tuple-element.19), channel_id=1, source_target_pairs={{0,8},{8,16},{16,24},{1,9},{9,17},{17,25},{2,10},{10,18},{18,26},{... | collective-permute-start | bytes 98312 | tf_op jit(solution)/shard_map/ppermute | solution.py:183
  4.3 2.2 %collective-permute-start.1 = (bf16[8,1,2048]{2,1,0:T(2,128)(2,1)S(1)}, bf16[8,1,2048]{2,1,0:T(2,128)(2,1)S(1)}, u32[]{:S(2)}, u32[]{:S(2)}) collective-permute-start(bf16[8,1,2048]{2,1,0:T(2,128)(2,1)S(1)} %get-tuple-element.18), channel_id=1, source_target_pairs={{8,0},{16,8},{24,16},{9,1},{17,9},{25,17},{10,2},{18,10},{26,18},{... | collective-permute-start | bytes 98312 | tf_op jit(solution)/shard_map/ppermute | solution.py:184
  6.4 0.7 fusion.9
  7.3 0.7 multiply_bitcast_fusion.1
  8.0 1.0 multiply_convert_fusion
  8.9 0.7 mul.248
  9.6 0.4 copy.48
  10.6 0.2 pad_maximum_fusion.lhs_ref
  10.9 0.4 copy-done.7
  11.5 0.3 copy-done
  11.9 38.8 %march.1 = f32[4,4,8,2048]{3,2,1,0:T(8,128)S(1)} custom-call(s32[16]{0:T(128)S(1)} %bitcast.130, bf16[8,32,2048]{2,1,0:T(8,128)(2,1)S(1)} %copy-done, bf16[8,1,2048]{2,1,0:T(2,128)(2,1)S(1)} %collective-permute-done.above_ref, bf16[8,1,2048]{2,1,0:T(2,128)(2,1)S(1)} %collective-permute-done.1.below_ref, bf16[8,256,144]{2,1,0:T(8,128)(2,1)S(1)} %pad_maximum_fusion.lhs_ref, ...), custom_call_target="tpu_custom_call" | custom-call | tf_op jit(solution)/shard_map/march/pallas_call | solution.py:154
  50.8 0.5 copy-done.8
  51.3 0.6 dynamic_slice.3
  52.5 0.2 collective-permute-done.2
  53.0 10.1 %collective-permute-start.3 = (f32[4,1,8,2048]{3,2,0,1:T(8,128)S(1)}, f32[4,1,8,2048]{3,2,0,1:T(8,128)S(1)}, u32[]{:S(2)}, u32[]{:S(2)}) collective-permute-start(f32[4,1,8,2048]{3,2,0,1:T(8,128)S(1)} %select_bitcast_fusion.1), channel_id=1, source_target_pairs={{0,2},{2,0},{1,3},{3,1},{4,6},{6,4},{5,7},{7,5},{8,10},{10,8},{9,1... | collective-permute-start | bytes 786440 | tf_op jit(solution)/shard_map/ppermute | solution.py:35
  63.7 5.7 %collective-permute-done.3 = f32[4,1,8,2048]{3,2,0,1:T(8,128)S(1)} collective-permute-done((f32[4,1,8,2048]{3,2,0,1:T(8,128)S(1)}, f32[4,1,8,2048]{3,2,0,1:T(8,128)S(1)}, u32[]{:S(2)}, u32[]{:S(2)}) %collective-permute-start.3) | collective-permute-done | bytes 262176 | tf_op jit(solution)/shard_map/ppermute | solution.py:35
  69.6 28.1 %collective-permute-start.4 = (f32[4,1,4,2048]{3,2,0,1:T(4,128)S(1)}, f32[4,1,4,2048]{3,2,0,1:T(4,128)S(1)}, u32[]{:S(2)}, u32[]{:S(2)}) collective-permute-start(f32[4,1,4,2048]{3,2,0,1:T(4,128)S(1)} %select_bitcast_fusion.2), channel_id=1, source_target_pairs={{0,4},{4,0},{1,5},{5,1},{2,6},{6,2},{3,7},{7,3},{8,12},{12,8},{9,1... | collective-permute-start | bytes 393224 | tf_op jit(solution)/shard_map/ppermute | solution.py:35
  98.4 6.1 %collective-permute-done.4 = f32[4,1,4,2048]{3,2,0,1:T(4,128)S(1)} collective-permute-done((f32[4,1,4,2048]{3,2,0,1:T(4,128)S(1)}, f32[4,1,4,2048]{3,2,0,1:T(4,128)S(1)}, u32[]{:S(2)}, u32[]{:S(2)}) %collective-permute-start.4) | collective-permute-done | bytes 131104 | tf_op jit(solution)/shard_map/ppermute | solution.py:35
  104.7 2.2 %collective-permute-start.5 = (f32[3,1,1,2048]{3,1,0,2:T(1,128)S(1)}, f32[3,1,1,2048]{3,1,0,2:T(1,128)S(1)}, u32[]{:S(2)}, u32[]{:S(2)}) collective-permute-start(f32[3,1,1,2048]{3,1,0,2:T(1,128)S(1)} %get-tuple-element.35), channel_id=1, source_target_pairs={{0,8},{8,16},{16,24},{24,0},{1,9},{9,17},{17,25},{25,1},{2,10},{10... | collective-permute-start | bytes 73736 | tf_op jit(solution)/shard_map/ppermute | solution.py:19
  106.9 0.9 collective-permute-done.5
  107.8 2.6 %collective-permute-done.6 = f32[3,1,1,2048]{3,1,0,2:T(1,128)S(1)} collective-permute-done((f32[3,1,1,2048]{3,1,0,2:T(1,128)S(1)}, f32[3,1,1,2048]{3,1,0,2:T(1,128)S(1)}, u32[]{:S(2)}, u32[]{:S(2)}) %collective-permute-start.6) | collective-permute-done | bytes 24608 | tf_op jit(solution)/shard_map/ppermute | solution.py:21
  110.5 4.2 %collective-permute-start.7 = (f32[3,6,1,2048]{3,1,0,2:T(8,128)S(1)}, f32[3,6,1,2048]{3,1,0,2:T(8,128)S(1)}, u32[]{:S(2)}, u32[]{:S(2)}) collective-permute-start(f32[3,6,1,2048]{3,1,0,2:T(8,128)S(1)} %pad_maximum_fusion.2), channel_id=1, source_target_pairs={{0,1},{1,2},{2,3},{3,4},{4,5},{5,6},{6,7},{7,0},{8,9},{9,10},{10,1... | collective-permute-start | bytes 442376 | tf_op jit(solution)/shard_map/ppermute | solution.py:19
  114.8 0.3 slice_reduce_fusion.8
  115.1 4.0 %collective-permute-done.7 = f32[3,6,1,2048]{3,1,0,2:T(8,128)S(1)} collective-permute-done((f32[3,6,1,2048]{3,1,0,2:T(8,128)S(1)}, f32[3,6,1,2048]{3,1,0,2:T(8,128)S(1)}, u32[]{:S(2)}, u32[]{:S(2)}) %collective-permute-start.7) | collective-permute-done | bytes 147488 | tf_op jit(solution)/shard_map/ppermute | solution.py:19
  119.2 2.5 %collective-permute-done.8 = f32[3,6,1,2048]{3,1,0,2:T(8,128)S(1)} collective-permute-done((f32[3,6,1,2048]{3,1,0,2:T(8,128)S(1)}, f32[3,6,1,2048]{3,1,0,2:T(8,128)S(1)}, u32[]{:S(2)}, u32[]{:S(2)}) %collective-permute-start.8) | collective-permute-done | bytes 147488 | tf_op jit(solution)/shard_map/ppermute | solution.py:21
  121.9 0.2 pad_slice_fusion.5
  122.1 0.3 pad_slice_fusion.1
  122.3 0.2 multiply_reduce_fusion.1
  123.3 0.2 multiply_reduce_fusion.6
  123.5 0.2 bitcast_add_fusion
  123.7 0.7 copy.55
  (62 shorter events, 2.8 us)
Async XLA Ops:
  1.1 10.3 %collective-permute-start = (bf16[8,1,2048]{2,1,0:T(2,128)(2,1)S(1)}, bf16[8,1,2048]{2,1,0:T(2,128)(2,1)S(1)}, u32[]{:S(2)}, u32[]{:S(2)}) collective-permute-start(bf16[8,1,2048]{2,1,0:T(2,128)(2,1)S(1)} %get-tuple-element.19), channel_id=1, source_target_pairs={{0,8},{8,16},{16,24},{1,9},{9,17},{17,25},{2,10},{10,18},{18,26},{... | collective-permute-start | bytes 98312 | tf_op jit(solution)/shard_map/ppermute | solution.py:183
  4.3 7.2 %collective-permute-start.1 = (bf16[8,1,2048]{2,1,0:T(2,128)(2,1)S(1)}, bf16[8,1,2048]{2,1,0:T(2,128)(2,1)S(1)}, u32[]{:S(2)}, u32[]{:S(2)}) collective-permute-start(bf16[8,1,2048]{2,1,0:T(2,128)(2,1)S(1)} %get-tuple-element.18), channel_id=1, source_target_pairs={{8,0},{16,8},{24,16},{9,1},{17,9},{25,17},{10,2},{18,10},{26,18},{... | collective-permute-start | bytes 98312 | tf_op jit(solution)/shard_map/ppermute | solution.py:184
  8.9 1.1 copy-start.3
  9.6 0.7 copy-start.4
  9.6 0.7 copy-start.6
  10.6 0.7 copy-start.7
  10.6 1.2 copy-start
  10.6 1.2 copy-start.1
  50.6 0.7 copy-start.8
  50.7 2.0 %collective-permute-start.2 = (f32[4,2,8,2048]{3,2,0,1:T(8,128)S(1)}, f32[4,2,8,2048]{3,2,0,1:T(8,128)S(1)}, u32[]{:S(2)}, u32[]{:S(2)}) collective-permute-start(f32[4,2,8,2048]{3,2,0,1:T(8,128)S(1)} %select_bitcast_fusion), channel_id=1, source_target_pairs={{0,1},{1,0},{2,3},{3,2},{4,5},{5,4},{6,7},{7,6},{8,9},{9,8},{10,11... | collective-permute-start | bytes 1572872 | tf_op jit(solution)/shard_map/ppermute | solution.py:35
  53.0 16.4 %collective-permute-start.3 = (f32[4,1,8,2048]{3,2,0,1:T(8,128)S(1)}, f32[4,1,8,2048]{3,2,0,1:T(8,128)S(1)}, u32[]{:S(2)}, u32[]{:S(2)}) collective-permute-start(f32[4,1,8,2048]{3,2,0,1:T(8,128)S(1)} %select_bitcast_fusion.1), channel_id=1, source_target_pairs={{0,2},{2,0},{1,3},{3,1},{4,6},{6,4},{5,7},{7,5},{8,10},{10,8},{9,1... | collective-permute-start | bytes 786440 | tf_op jit(solution)/shard_map/ppermute | solution.py:35
  69.6 45.3 %copy-start.2 = (f32[3,3,3,3]{3,2,1,0:T(4,128)S(1)}, f32[3,3,3,3]{3,2,1,0:T(4,128)}, u32[]{:S(2)}) copy-start(f32[3,3,3,3]{3,2,1,0:T(4,128)} %param.19) | copy-start | bytes 976
  69.6 34.9 %collective-permute-start.4 = (f32[4,1,4,2048]{3,2,0,1:T(4,128)S(1)}, f32[4,1,4,2048]{3,2,0,1:T(4,128)S(1)}, u32[]{:S(2)}, u32[]{:S(2)}) collective-permute-start(f32[4,1,4,2048]{3,2,0,1:T(4,128)S(1)} %select_bitcast_fusion.2), channel_id=1, source_target_pairs={{0,4},{4,0},{1,5},{5,1},{2,6},{6,2},{3,7},{7,3},{8,12},{12,8},{9,1... | collective-permute-start | bytes 393224 | tf_op jit(solution)/shard_map/ppermute | solution.py:35
  104.7 3.1 %collective-permute-start.5 = (f32[3,1,1,2048]{3,1,0,2:T(1,128)S(1)}, f32[3,1,1,2048]{3,1,0,2:T(1,128)S(1)}, u32[]{:S(2)}, u32[]{:S(2)}) collective-permute-start(f32[3,1,1,2048]{3,1,0,2:T(1,128)S(1)} %get-tuple-element.35), channel_id=1, source_target_pairs={{0,8},{8,16},{16,24},{24,0},{1,9},{9,17},{17,25},{25,1},{2,10},{10... | collective-permute-start | bytes 73736 | tf_op jit(solution)/shard_map/ppermute | solution.py:19
  106.9 3.6 %collective-permute-start.6 = (f32[3,1,1,2048]{3,1,0,2:T(1,128)S(1)}, f32[3,1,1,2048]{3,1,0,2:T(1,128)S(1)}, u32[]{:S(2)}, u32[]{:S(2)}) collective-permute-start(f32[3,1,1,2048]{3,1,0,2:T(1,128)S(1)} %get-tuple-element.36), channel_id=1, source_target_pairs={{8,0},{16,8},{24,16},{0,24},{9,1},{17,9},{25,17},{1,25},{10,2},{18... | collective-permute-start | bytes 73736 | tf_op jit(solution)/shard_map/ppermute | solution.py:21
  110.5 8.6 %collective-permute-start.7 = (f32[3,6,1,2048]{3,1,0,2:T(8,128)S(1)}, f32[3,6,1,2048]{3,1,0,2:T(8,128)S(1)}, u32[]{:S(2)}, u32[]{:S(2)}) collective-permute-start(f32[3,6,1,2048]{3,1,0,2:T(8,128)S(1)} %pad_maximum_fusion.2), channel_id=1, source_target_pairs={{0,1},{1,2},{2,3},{3,4},{4,5},{5,6},{6,7},{7,0},{8,9},{9,10},{10,1... | collective-permute-start | bytes 442376 | tf_op jit(solution)/shard_map/ppermute | solution.py:19
  114.8 6.9 %collective-permute-start.8 = (f32[3,6,1,2048]{3,1,0,2:T(8,128)S(1)}, f32[3,6,1,2048]{3,1,0,2:T(8,128)S(1)}, u32[]{:S(2)}, u32[]{:S(2)}) collective-permute-start(f32[3,6,1,2048]{3,1,0,2:T(8,128)S(1)} %pad_maximum_fusion.2), channel_id=1, source_target_pairs={{1,0},{2,1},{3,2},{4,3},{5,4},{6,5},{7,6},{0,7},{9,8},{10,9},{11,1... | collective-permute-start | bytes 442376 | tf_op jit(solution)/shard_map/ppermute | solution.py:21
  122.3 1.2 copy-start.5

commit v2 on v1

--- a/solution.py
+++ b/solution.py
@@ -7,23 +7,6 @@
 from jax.experimental import pallas as pl
 from jax.experimental.pallas import tpu as pltpu
 from jax.sharding import PartitionSpec as P
-
-def with_halo(cells, sides, width, closed):
-    for axis, dim in sides:
-        count = lax.axis_size(axis)
-        ends = count if closed else count - 1
-        head = lax.slice_in_dim(cells, 0, width, axis=dim)
-        tail = lax.slice_in_dim(cells, cells.shape[dim] - width, cells.shape[dim], axis=dim)
-        cells = jnp.concatenate(
-            [
-                lax.ppermute(tail, axis, [(i, (i + 1) % count) for i in range(ends)]),
-                cells,
-                lax.ppermute(head, axis, [((i + 1) % count, i) for i in range(ends)]),
-            ],
-            axis=dim,
-        )
-    return cells
-
 
 def partner(block, axis, stride):
     count = lax.axis_size(axis)
@@ -38,7 +21,7 @@
 LANES = 128
 
 
-def march_kernel(optical, unroll, occ_ref, vol_ref, above_ref, below_ref, lhs_ref, mix_ref, bias_ref, out_ref, feat, picks):
+def march_kernel(optical, unroll, group, occ_ref, vol_ref, above_ref, below_ref, lhs_ref, mix_ref, bias_ref, out_ref, feat, picks):
     layers, rows, cols = vol_ref.shape
     bricks = occ_ref.shape[0]
     tiles = out_ref.shape[0]
@@ -74,47 +57,53 @@
     found = lax.fori_loop(0, bricks, pick, 0)
 
     def pair(step, carry):
-        part = step // tiles
-        tile = step % tiles
+        part = step // (tiles // group)
+        first_tile = step % (tiles // group) * group
         low = pl.ds(pl.multiple_of(picks[2 * part] * LANES, LANES), LANES)
         high = pl.ds(pl.multiple_of(picks[jnp.minimum(2 * part + 1, found - 1)] * LANES, LANES), LANES)
 
-        def layer(z, state):
-            colour, remaining = state
+        def layer(z, states):
             x = jnp.concatenate([feat[z, :, low], feat[z, :, high]], 1)
-            out = bias_ref[...]
-            for p in range(2):
-                u = jnp.dot(lhs_ref[2 * tile + p], x, preferred_element_type=jnp.float32)
-                hidden = (u + u * jnp.tanh(u)).astype(jnp.bfloat16)
-                out = out + jnp.dot(mix_ref[p], hidden, preferred_element_type=jnp.float32)
-            raw = out[24:32]
-            density = jnp.maximum(raw, 0.0) + jnp.log1p(jnp.exp(-jnp.abs(raw)))
-            keep = jnp.exp(-optical * density)
-            weight = 0.5 * (remaining * (1.0 - keep))
-            colour = tuple(
-                colour[i] + (weight + weight * jnp.tanh(out[8 * i:8 * i + 8])) for i in range(3)
-            )
-            return colour, remaining * keep
+            lhs = lhs_ref[pl.ds(first_tile, group)].reshape(-1, lhs_ref.shape[2])
+            us = jnp.dot(lhs, x, preferred_element_type=jnp.float32)
+            fresh = []
+            span = us.shape[0] // group // 2
+            for t, (colour, remaining) in enumerate(states):
+                out = bias_ref[...]
+                for p in range(2):
+                    at = (2 * t + p) * span
+                    u = us[at:at + span]
+                    hidden = (u + u * jnp.tanh(u)).astype(jnp.bfloat16)
+                    out = out + jnp.dot(mix_ref[p], hidden, preferred_element_type=jnp.float32)
+                raw = out[24:32]
+                density = jnp.maximum(raw, 0.0) + jnp.log1p(jnp.exp(-jnp.abs(raw)))
+                keep = jnp.exp(-optical * density)
+                weight = 0.5 * (remaining * (1.0 - keep))
+                colour = tuple(
+                    colour[i] + (weight + weight * jnp.tanh(out[8 * i:8 * i + 8])) for i in range(3)
+                )
+                fresh.append((colour, remaining * keep))
+            return tuple(fresh)
 
         zero = jnp.zeros((8, 2 * LANES), jnp.float32)
-        state = ((zero, zero, zero), jnp.ones((8, 2 * LANES), jnp.float32))
-
-        def layer_group(group, state):
+        states = (((zero, zero, zero), jnp.ones((8, 2 * LANES), jnp.float32)),) * group
+
+        def layer_group(step_z, states):
             for k in range(unroll):
-                state = layer(group * unroll + k, state)
-            return state
+                states = layer(step_z * unroll + k, states)
+            return states
 
         if unroll == layers:
-            state = layer_group(0, state)
+            states = layer_group(0, states)
         else:
-            state = lax.fori_loop(0, layers // unroll, layer_group, state)
-        colour, remaining = state
-        for i, value in enumerate(colour + (remaining,)):
-            out_ref[tile, i, :, low] = value[:, :LANES]
-            out_ref[tile, i, :, high] = value[:, LANES:]
+            states = lax.fori_loop(0, layers // unroll, layer_group, states)
+        for t, (colour, remaining) in enumerate(states):
+            for i, value in enumerate(colour + (remaining,)):
+                out_ref[first_tile + t, i, :, low] = value[:, :LANES]
+                out_ref[first_tile + t, i, :, high] = value[:, LANES:]
         return carry
 
-    lax.fori_loop(0, (found + 1) // 2 * tiles, pair, 0)
+    lax.fori_loop(0, (found + 1) // 2 * (tiles // group), pair, 0)
 
 
 def march(volume, above, below, occupancy, w_in, b_in, w_out, b_out, depth_count, optical):
@@ -140,7 +129,7 @@
     parts = jnp.stack(parts + [jnp.zeros_like(b_in)] * 13, 1)
     parts = jnp.broadcast_to(parts[None], (rows, hidden, 16)).reshape(rows * hidden, 16)
     lhs = jnp.concatenate([spread, parts], 1).astype(jnp.bfloat16)
-    lhs = lhs.reshape(2 * tiles, 4 * hidden, channels * rows + 16)
+    lhs = lhs.reshape(tiles, 8 * hidden, channels * rows + 16)
     scale = jnp.asarray(np.array([0.5, 0.5, 0.5, 1.0], np.float32))
     place = np.zeros((2, 8, 4), np.float32)
     for p in range(2):
@@ -152,7 +141,7 @@
     bias = jnp.broadcast_to((b_out * scale)[:, None, None], (4, 8, 2 * LANES)).reshape(32, 2 * LANES)
     vmem = pl.BlockSpec(memory_space=pltpu.VMEM)
     return pl.pallas_call(
-        functools.partial(march_kernel, optical, 8),
+        functools.partial(march_kernel, optical, layers, tiles),
         out_shape=jax.ShapeDtypeStruct((tiles, 4, 8, cols), jnp.float32),
         in_specs=[pl.BlockSpec(memory_space=pltpu.SMEM)] + [vmem] * 6,
         out_specs=vmem,
@@ -175,7 +164,6 @@
     depth_count = lax.axis_size("depth")
     depth_index = lax.axis_index("depth")
     strip_count = lax.axis_size("strip")
-    strip_index = lax.axis_index("strip")
     layers, rows_here, columns = volume.shape
     optical = 2.0 / (layers * depth_count)
     down_route = [(i, i + 1) for i in range(strip_count - 1)]
@@ -206,26 +194,27 @@
         if paired.shape[3] == row_share and tiles >> (bit_index + 1) < 1:
             composed = composed.reshape(4, 1, -1, columns)
     composed = composed.reshape(4, row_share, columns)
-    picture = composed[:3][:, :, None, :]
-    extended = with_halo(picture, (("strip", 1), ("depth", 2)), 1, True)
-    edge_weight = jnp.concatenate(
-        [
-            (strip_index > 0).astype(jnp.float32)[None],
-            jnp.ones((row_share,), jnp.float32),
-            (strip_index < strip_count - 1).astype(jnp.float32)[None],
-        ],
-        0,
-    )
-    extended = extended * edge_weight[None, :, None, None]
-    row_centre = extended[:, 1 : row_share + 1, 1]
+    picture = composed[:3]
+    ring = [(i, (i + 1) % depth_count) for i in range(depth_count)]
+    back = [(j, i) for i, j in ring]
+    last = depth_count - 1
+    corner = [(i * depth_count + last, (i + 1) * depth_count) for i in range(strip_count - 1)]
+    corner_back = [(j, i) for i, j in corner]
+    from_above = lax.ppermute(picture, "depth", ring)
+    from_below = lax.ppermute(picture, "depth", back)
+    strip_above = lax.ppermute(picture[:, row_share - 1 :], ("strip", "depth"), corner)
+    strip_below = lax.ppermute(picture[:, :1], ("strip", "depth"), corner_back)
     row_above = jnp.where(
-        depth_index == 0, extended[:, 0:row_share, 0], extended[:, 1 : row_share + 1, 0]
+        depth_index == 0,
+        jnp.concatenate([strip_above, from_above[:, : row_share - 1]], 1),
+        from_above,
     )
     row_below = jnp.where(
-        depth_index == depth_count - 1,
-        extended[:, 2 : row_share + 2, 2],
-        extended[:, 1 : row_share + 1, 2],
-    )
+        depth_index == last,
+        jnp.concatenate([from_below[:, 1:], strip_below], 1),
+        from_below,
+    )
+    row_centre = picture
     row_sets = [row_above, row_centre, row_below]
     filtered = jnp.broadcast_to(conv_bias[:, None, None], (3, row_share, columns))
     for row_off in range(3):

time: 126 us -> 97.8 us (0.78); the launches traced: 124 us -> 98.1 us
  Pallas kernels: 38.8 us -> 19.8 us
  starting transfers between devices: 50 us -> 46.7 us
  waiting for transfers between devices: 22 us -> 18.8 us
    pallas_call x1, Pallas kernels: 38.8 us -> 19.8 us  [march(): pl.pallas_call(functools.partial(march_kernel, optical, layers, tiles), o...]
    ppermute x3, starting transfers between devices: 38.3 us -> 23.1 us  [partner(): return lax.ppermute(block, axis, route)]
    ppermute x4, starting transfers between devices: 6.41 us -> 18.3 us  [the longest x1 12.3 us: shards(): lax.ppermute(picture[:, row_share - 1:], ('strip', 'depth'), corner)]
    ppermute x4, waiting for transfers between devices: 10.1 us -> 6.78 us  [the longest x1 6.77 us: shards(): strip_below = lax.ppermute(picture[:, :1], ('strip', 'depth'), corner_back)]
  transfers between devices with their start and end apart: 9 -> 9, of which waited for: 7 -> 4; matrix products, arithmetic and copies ran while one was open for 4% -> 6% of each run, Pallas kernels for 0% -> 0%
where the time goes in v2:
time: 97.8 us; the launch traced here: 98.1 us
  starting transfers between devices  46.7 us (48%)
  Pallas kernels  19.8 us (20%)
  waiting for transfers between devices  18.8 us (19%)
  local copies, waits for them, and re-layouts  6 us (6%)
  other arithmetic  4.47 us (5%)
  between operations  2.4 us (2%)
    ppermute x3, starting transfers between devices, partner(): return lax.ppermute(block, axis, route)  23.1 us
    pallas_call x1, Pallas kernels, march(): pl.pallas_call(functools.partial(march_kernel, optical, layers, tiles), o...  19.8 us
    ppermute x1, starting transfers between devices, shards(): lax.ppermute(picture[:, row_share - 1:], ('strip', 'depth'), corner)  12.3 us
    ppermute x3, waiting for transfers between devices, partner(): return lax.ppermute(block, axis, route)  12 us
    ppermute x1, waiting for transfers between devices, shards(): strip_below = lax.ppermute(picture[:, :1], ('strip', 'depth'), corner_back)  6.77 us
    ppermute x1, starting transfers between devices, shards(): from_above = lax.ppermute(picture, 'depth', ring)  4.59 us
    ppermute x1, starting transfers between devices, shards(): above = lax.ppermute(volume[:, rows_here - 1:], 'strip', down_route)  3.12 us
    ppermute x1, starting transfers between devices, shards(): below = lax.ppermute(volume[:, :1], 'strip', up_route)  2.16 us
  transfers between devices with their start and end apart: 9, of which 4 were waited for; matrix products, arithmetic and copies ran while one was open for 6% of the time, Pallas kernels for 0%

profile of v2, /device:TPU:27, one launch (start us, length us, event | category | flops | bytes accessed | tf_op | source)
XLA Modules:
  0.0 98.1 jit_solution(8054641494577657427)
XLA Ops:
  0.0 1.1 %fusion.8 = (bf16[8,1,2048]{2,1,0:T(2,128)(2,1)S(1)}, bf16[8,1,2048]{2,1,0:T(2,128)(2,1)S(1)}) fusion(bf16[8,32,2048]{2,1,0:T(8,128)(2,1)} %vol_ref.1), kind=kLoop, calls=%fused_computation.75 | loop fusion | bytes 131072 | tf_op jit(solution)/shard_map/slice | solution.py:172
  1.1 3.1 %collective-permute-start = (bf16[8,1,2048]{2,1,0:T(2,128)(2,1)S(1)}, bf16[8,1,2048]{2,1,0:T(2,128)(2,1)S(1)}, u32[]{:S(2)}, u32[]{:S(2)}) collective-permute-start(bf16[8,1,2048]{2,1,0:T(2,128)(2,1)S(1)} %get-tuple-element.19), channel_id=1, source_target_pairs={{0,8},{8,16},{16,24},{1,9},{9,17},{17,25},{2,10},{10,18},{18,26},{... | collective-permute-start | bytes 98312 | tf_op jit(solution)/shard_map/ppermute | solution.py:171
  4.3 2.2 %collective-permute-start.1 = (bf16[8,1,2048]{2,1,0:T(2,128)(2,1)S(1)}, bf16[8,1,2048]{2,1,0:T(2,128)(2,1)S(1)}, u32[]{:S(2)}, u32[]{:S(2)}) collective-permute-start(bf16[8,1,2048]{2,1,0:T(2,128)(2,1)S(1)} %get-tuple-element.18), channel_id=1, source_target_pairs={{8,0},{16,8},{24,16},{9,1},{17,9},{25,17},{10,2},{18,10},{26,18},{... | collective-permute-start | bytes 98312 | tf_op jit(solution)/shard_map/ppermute | solution.py:172
  6.4 0.7 fusion.7
  7.3 0.7 multiply_bitcast_fusion.1
  8.0 1.0 multiply_convert_fusion
  8.9 0.6 mul.240
  9.5 0.4 copy.48
  10.5 0.2 pad_maximum_fusion.lhs_ref
  10.8 0.4 copy-done.7
  11.4 0.3 copy-done
  11.8 19.8 %march.1 = f32[4,4,8,2048]{3,2,1,0:T(8,128)S(1)} custom-call(s32[16]{0:T(128)S(1)} %bitcast.123, bf16[8,32,2048]{2,1,0:T(8,128)(2,1)S(1)} %copy-done, bf16[8,1,2048]{2,1,0:T(2,128)(2,1)S(1)} %collective-permute-done.above_ref, bf16[8,1,2048]{2,1,0:T(2,128)(2,1)S(1)} %collective-permute-done.1.below_ref, bf16[4,512,144]{2,1,0:T(8,128)(2,1)S(1)} %pad_maximum_fusion.lhs_ref, ...), custom_call_target="tpu_custom_call" | custom-call | tf_op jit(solution)/shard_map/march/pallas_call | solution.py:143
  31.6 12.6 %collective-permute-start.2 = (f32[4,2,8,2048]{3,2,0,1:T(8,128)S(1)}, f32[4,2,8,2048]{3,2,0,1:T(8,128)S(1)}, u32[]{:S(2)}, u32[]{:S(2)}) collective-permute-start(f32[4,2,8,2048]{3,2,0,1:T(8,128)S(1)} %select_bitcast_fusion), channel_id=1, source_target_pairs={{0,1},{1,0},{2,3},{3,2},{4,5},{5,4},{6,7},{7,6},{8,9},{9,8},{10,11... | collective-permute-start | bytes 1572872 | tf_op jit(solution)/shard_map/ppermute | solution.py:18
  44.2 0.6 dynamic_slice.3
  45.5 0.3 collective-permute-done.2
  46.8 6.8 %collective-permute-done.3 = f32[4,1,8,2048]{3,2,0,1:T(8,128)S(1)} collective-permute-done((f32[4,1,8,2048]{3,2,0,1:T(8,128)S(1)}, f32[4,1,8,2048]{3,2,0,1:T(8,128)S(1)}, u32[]{:S(2)}, u32[]{:S(2)}) %collective-permute-start.3) | collective-permute-done | bytes 262176 | tf_op jit(solution)/shard_map/ppermute | solution.py:18
  53.9 10.4 %collective-permute-start.4 = (f32[4,1,4,2048]{3,2,0,1:T(4,128)S(1)}, f32[4,1,4,2048]{3,2,0,1:T(4,128)S(1)}, u32[]{:S(2)}, u32[]{:S(2)}) collective-permute-start(f32[4,1,4,2048]{3,2,0,1:T(4,128)S(1)} %select_bitcast_fusion.2), channel_id=1, source_target_pairs={{0,4},{4,0},{1,5},{5,1},{2,6},{6,2},{3,7},{7,3},{8,12},{12,8},{9,1... | collective-permute-start | bytes 393224 | tf_op jit(solution)/shard_map/ppermute | solution.py:18
  65.0 0.3 slice_reduce_fusion.8
  65.3 4.9 %collective-permute-done.4 = f32[4,1,4,2048]{3,2,0,1:T(4,128)S(1)} collective-permute-done((f32[4,1,4,2048]{3,2,0,1:T(4,128)S(1)}, f32[4,1,4,2048]{3,2,0,1:T(4,128)S(1)}, u32[]{:S(2)}, u32[]{:S(2)}) %collective-permute-start.4) | collective-permute-done | bytes 131104 | tf_op jit(solution)/shard_map/ppermute | solution.py:18
  70.3 4.6 %collective-permute-start.6 = (f32[3,4,2048]{2,1,0:T(4,128)S(1)}, f32[3,4,2048]{2,1,0:T(4,128)S(1)}, u32[]{:S(2)}, u32[]{:S(2)}) collective-permute-start(f32[3,4,2048]{2,1,0:T(4,128)S(1)} %fusion.5), channel_id=1, source_target_pairs={{0,1},{1,2},{2,3},{3,4},{4,5},{5,6},{6,7},{7,0},{8,9},{9,10},{10,1... | collective-permute-start | bytes 294920 | tf_op jit(solution)/shard_map/ppermute | solution.py:203
  74.9 0.2 pad_slice_fusion.3
  75.2 12.3 %collective-permute-start.5 = (f32[3,1,2048]{2,1,0:T(1,128)S(1)}, f32[3,1,2048]{2,1,0:T(1,128)S(1)}, u32[]{:S(2)}, u32[]{:S(2)}) collective-permute-start(f32[3,1,2048]{2,1,0:T(1,128)S(1)} %get-tuple-element.28), channel_id=1, source_target_pairs={{7,8},{15,16},{23,24}} | collective-permute-start | bytes 73736 | tf_op jit(solution)/shard_map/ppermute | solution.py:205
  87.5 1.3 %collective-permute-start.8 = (f32[3,1,2048]{2,1,0:T(1,128)S(1)}, f32[3,1,2048]{2,1,0:T(1,128)S(1)}, u32[]{:S(2)}, u32[]{:S(2)}) collective-permute-start(f32[3,1,2048]{2,1,0:T(1,128)S(1)} %get-tuple-element.29), channel_id=1, source_target_pairs={{8,7},{16,15},{24,23}} | collective-permute-start | bytes 73736 | tf_op jit(solution)/shard_map/ppermute | solution.py:206
  88.8 0.2 multiply_reduce_fusion.3
  89.2 0.2 pad_slice_fusion.5
  89.5 6.8 %collective-permute-done.8 = f32[3,1,2048]{2,1,0:T(1,128)S(1)} collective-permute-done((f32[3,1,2048]{2,1,0:T(1,128)S(1)}, f32[3,1,2048]{2,1,0:T(1,128)S(1)}, u32[]{:S(2)}, u32[]{:S(2)}) %collective-permute-start.8) | collective-permute-done | bytes 24608 | tf_op jit(solution)/shard_map/ppermute | solution.py:206
  96.3 0.2 pad_slice_fusion.1
  96.5 0.1 multiply_reduce_fusion.1
  96.7 0.2 multiply_reduce_fusion.6
  97.0 0.2 multiply_reduce_fusion
  97.2 0.2 bitcast_add_fusion
  97.3 0.7 copy.55
  (60 shorter events, 2.2 us)
Async XLA Ops:
  1.1 10.2 %collective-permute-start = (bf16[8,1,2048]{2,1,0:T(2,128)(2,1)S(1)}, bf16[8,1,2048]{2,1,0:T(2,128)(2,1)S(1)}, u32[]{:S(2)}, u32[]{:S(2)}) collective-permute-start(bf16[8,1,2048]{2,1,0:T(2,128)(2,1)S(1)} %get-tuple-element.19), channel_id=1, source_target_pairs={{0,8},{8,16},{16,24},{1,9},{9,17},{17,25},{2,10},{10,18},{18,26},{... | collective-permute-start | bytes 98312 | tf_op jit(solution)/shard_map/ppermute | solution.py:171
  4.3 7.1 %collective-permute-start.1 = (bf16[8,1,2048]{2,1,0:T(2,128)(2,1)S(1)}, bf16[8,1,2048]{2,1,0:T(2,128)(2,1)S(1)}, u32[]{:S(2)}, u32[]{:S(2)}) collective-permute-start(bf16[8,1,2048]{2,1,0:T(2,128)(2,1)S(1)} %get-tuple-element.18), channel_id=1, source_target_pairs={{8,0},{16,8},{24,16},{9,1},{17,9},{25,17},{10,2},{18,10},{26,18},{... | collective-permute-start | bytes 98312 | tf_op jit(solution)/shard_map/ppermute | solution.py:172
  8.9 1.0 %copy-start.3 = (f32[2,8,4]{2,1,0:T(8,128)S(1)}, f32[2,8,4]{2,1,0:T(8,128)}, u32[]{:S(2)}) copy-start(f32[2,8,4]{2,1,0:T(8,128)} %constant.43.clone) | copy-start | bytes 772
  9.5 0.7 copy-start.4
  9.5 0.7 copy-start.6
  10.5 0.7 copy-start.7
  10.5 1.2 %copy-start = (bf16[8,32,2048]{2,1,0:T(8,128)(2,1)S(1)}, bf16[8,32,2048]{2,1,0:T(8,128)(2,1)}, u32[]{:S(2)}) copy-start(bf16[8,32,2048]{2,1,0:T(8,128)(2,1)} %vol_ref.1) | copy-start | bytes 3145732
  10.5 1.2 %copy-start.1 = (s32[1,1,16]{2,1,0:T(1,128)S(1)}, s32[1,1,16]{2,1,0:T(1,128)}, u32[]{:S(2)}) copy-start(s32[1,1,16]{2,1,0:T(1,128)} %param.13) | copy-start | bytes 196
  31.5 12.7 %copy-start.8 = (s32[8]{0:T(128)S(1)}, s32[8]{0:T(128)}, u32[]{:S(2)}) copy-start(s32[8]{0:T(128)} %param.14) | copy-start | bytes 100
  31.6 14.2 %collective-permute-start.2 = (f32[4,2,8,2048]{3,2,0,1:T(8,128)S(1)}, f32[4,2,8,2048]{3,2,0,1:T(8,128)S(1)}, u32[]{:S(2)}, u32[]{:S(2)}) collective-permute-start(f32[4,2,8,2048]{3,2,0,1:T(8,128)S(1)} %select_bitcast_fusion), channel_id=1, source_target_pairs={{0,1},{1,0},{2,3},{3,2},{4,5},{5,4},{6,7},{7,6},{8,9},{9,8},{10,11... | collective-permute-start | bytes 1572872 | tf_op jit(solution)/shard_map/ppermute | solution.py:18
  46.0 7.6 %collective-permute-start.3 = (f32[4,1,8,2048]{3,2,0,1:T(8,128)S(1)}, f32[4,1,8,2048]{3,2,0,1:T(8,128)S(1)}, u32[]{:S(2)}, u32[]{:S(2)}) collective-permute-start(f32[4,1,8,2048]{3,2,0,1:T(8,128)S(1)} %select_bitcast_fusion.1), channel_id=1, source_target_pairs={{0,2},{2,0},{1,3},{3,1},{4,6},{6,4},{5,7},{7,5},{8,10},{10,8},{9,1... | collective-permute-start | bytes 786440 | tf_op jit(solution)/shard_map/ppermute | solution.py:18
  53.7 11.3 %copy-start.2 = (f32[3,3,3,3]{3,2,1,0:T(4,128)S(1)}, f32[3,3,3,3]{3,2,1,0:T(4,128)}, u32[]{:S(2)}) copy-start(f32[3,3,3,3]{3,2,1,0:T(4,128)} %param.19) | copy-start | bytes 976
  53.9 16.3 %collective-permute-start.4 = (f32[4,1,4,2048]{3,2,0,1:T(4,128)S(1)}, f32[4,1,4,2048]{3,2,0,1:T(4,128)S(1)}, u32[]{:S(2)}, u32[]{:S(2)}) collective-permute-start(f32[4,1,4,2048]{3,2,0,1:T(4,128)S(1)} %select_bitcast_fusion.2), channel_id=1, source_target_pairs={{0,4},{4,0},{1,5},{5,1},{2,6},{6,2},{3,7},{7,3},{8,12},{12,8},{9,1... | collective-permute-start | bytes 393224 | tf_op jit(solution)/shard_map/ppermute | solution.py:18
  70.3 18.9 %collective-permute-start.6 = (f32[3,4,2048]{2,1,0:T(4,128)S(1)}, f32[3,4,2048]{2,1,0:T(4,128)S(1)}, u32[]{:S(2)}, u32[]{:S(2)}) collective-permute-start(f32[3,4,2048]{2,1,0:T(4,128)S(1)} %fusion.5), channel_id=1, source_target_pairs={{0,1},{1,2},{2,3},{3,4},{4,5},{5,6},{6,7},{7,0},{8,9},{9,10},{10,1... | collective-permute-start | bytes 294920 | tf_op jit(solution)/shard_map/ppermute | solution.py:203
  75.1 14.3 %collective-permute-start.7 = (f32[3,4,2048]{2,1,0:T(4,128)S(1)}, f32[3,4,2048]{2,1,0:T(4,128)S(1)}, u32[]{:S(2)}, u32[]{:S(2)}) collective-permute-start(f32[3,4,2048]{2,1,0:T(4,128)S(1)} %fusion.5), channel_id=1, source_target_pairs={{1,0},{2,1},{3,2},{4,3},{5,4},{6,5},{7,6},{0,7},{9,8},{10,9},{11,1... | collective-permute-start | bytes 294920 | tf_op jit(solution)/shard_map/ppermute | solution.py:204
  75.2 14.0 %collective-permute-start.5 = (f32[3,1,2048]{2,1,0:T(1,128)S(1)}, f32[3,1,2048]{2,1,0:T(1,128)S(1)}, u32[]{:S(2)}, u32[]{:S(2)}) collective-permute-start(f32[3,1,2048]{2,1,0:T(1,128)S(1)} %get-tuple-element.28), channel_id=1, source_target_pairs={{7,8},{15,16},{23,24}} | collective-permute-start | bytes 73736 | tf_op jit(solution)/shard_map/ppermute | solution.py:205
  87.5 8.7 %collective-permute-start.8 = (f32[3,1,2048]{2,1,0:T(1,128)S(1)}, f32[3,1,2048]{2,1,0:T(1,128)S(1)}, u32[]{:S(2)}, u32[]{:S(2)}) collective-permute-start(f32[3,1,2048]{2,1,0:T(1,128)S(1)} %get-tuple-element.29), channel_id=1, source_target_pairs={{8,7},{16,15},{24,23}} | collective-permute-start | bytes 73736 | tf_op jit(solution)/shard_map/ppermute | solution.py:206
  89.4 7.8 %copy-start.5 = (f32[3]{0:T(128)S(1)}, f32[3]{0:T(128)}, u32[]{:S(2)}) copy-start(f32[3]{0:T(128)} %param.20) | copy-start | bytes 40

commit v3 on v2

--- a/solution.py
+++ b/solution.py
@@ -21,7 +21,7 @@
 LANES = 128
 
 
-def march_kernel(optical, unroll, group, occ_ref, vol_ref, above_ref, below_ref, lhs_ref, mix_ref, bias_ref, out_ref, feat, picks):
+def march_kernel(optical, unroll, group, depth_count, occ_ref, vol_ref, above_ref, below_ref, pattern_ref, mix_ref, bias_ref, out_ref, feat, lhs_ref, picks):
     layers, rows, cols = vol_ref.shape
     bricks = occ_ref.shape[0]
     tiles = out_ref.shape[0]
@@ -47,6 +47,16 @@
         return carry
 
     lax.fori_loop(0, layers, features, 0)
+    pattern = pattern_ref[...]
+    hidden_size = pattern.shape[0]
+    source = lax.broadcasted_iota(jnp.int32, pattern.shape, 1)
+    source = jnp.where(source < 4 * rows, source % rows, -1)
+    share = rows // depth_count
+    for r in range(rows):
+        d, k = r % depth_count, r // depth_count
+        at = (d // tiles * share + k) * hidden_size
+        entry = jnp.where((source == r) | (source < 0), pattern, 0.0)
+        lhs_ref[d % tiles, at:at + hidden_size] = entry.astype(jnp.bfloat16)
     out_ref[:, :3] = jnp.zeros((tiles, 3, 8, cols), jnp.float32)
     out_ref[:, 3:] = jnp.ones((tiles, 1, 8, cols), jnp.float32)
 
@@ -111,25 +121,16 @@
     channels, hidden = w_in.shape
     tiles = rows // 8
     share = rows // depth_count
-    pos_row = np.zeros((tiles, 8), np.int64)
-    for r in range(rows):
-        d, k = r % depth_count, r // depth_count
-        pos_row[d % tiles, d // tiles * share + k] = r
-    chosen = np.zeros((rows, rows), np.float32)
-    chosen[np.arange(rows), pos_row.reshape(-1)] = 1.0
     half_in = 0.5 * w_in.astype(jnp.float32)
-    spread = jnp.asarray(chosen)[:, None, None, :] * half_in.T[None, :, :, None]
-    spread = spread.reshape(rows * hidden, channels * rows)
     rest = 0.5 * b_in
     parts = []
     for unused in range(3):
         part = lax.reduce_precision(rest, 8, 7)
         parts.append(part)
         rest = rest - part
-    parts = jnp.stack(parts + [jnp.zeros_like(b_in)] * 13, 1)
-    parts = jnp.broadcast_to(parts[None], (rows, hidden, 16)).reshape(rows * hidden, 16)
-    lhs = jnp.concatenate([spread, parts], 1).astype(jnp.bfloat16)
-    lhs = lhs.reshape(tiles, 8 * hidden, channels * rows + 16)
+    wide = jnp.repeat(half_in.T, rows, axis=1)
+    bias_in = jnp.pad(jnp.stack(parts, 1), ((0, 0), (0, 13)))
+    pattern = jnp.concatenate([wide, bias_in], 1)
     scale = jnp.asarray(np.array([0.5, 0.5, 0.5, 1.0], np.float32))
     place = np.zeros((2, 8, 4), np.float32)
     for p in range(2):
@@ -141,17 +142,18 @@
     bias = jnp.broadcast_to((b_out * scale)[:, None, None], (4, 8, 2 * LANES)).reshape(32, 2 * LANES)
     vmem = pl.BlockSpec(memory_space=pltpu.VMEM)
     return pl.pallas_call(
-        functools.partial(march_kernel, optical, layers, tiles),
+        functools.partial(march_kernel, optical, layers, tiles, depth_count),
         out_shape=jax.ShapeDtypeStruct((tiles, 4, 8, cols), jnp.float32),
         in_specs=[pl.BlockSpec(memory_space=pltpu.SMEM)] + [vmem] * 6,
         out_specs=vmem,
         scratch_shapes=[
             pltpu.VMEM((layers, channels * rows + 16, cols), jnp.bfloat16),
+            pltpu.VMEM((tiles, 8 * hidden, channels * rows + 16), jnp.bfloat16),
             pltpu.SMEM((occupancy.size + 1,), jnp.int32),
         ],
         compiler_params=pltpu.CompilerParams(vmem_limit_bytes=40 * 1024 * 1024),
         name="march",
-    )(occupancy.reshape(-1), volume, above, below, lhs, mix, bias)
+    )(occupancy.reshape(-1), volume, above, below, pattern, mix, bias)
 
 
 def over_pair(front_part, back_part):

time: 97.8 us -> 99.6 us (1.018)
  starting transfers between devices: 46.7 us -> 16.1 us
  Pallas kernels: 19.8 us -> 48.2 us
  waiting for transfers between devices: 18.8 us -> 21.8 us
    pallas_call x1, Pallas kernels: 19.8 us -> 48.2 us  [march(): pl.pallas_call(functools.partial(march_kernel, optical, layers, tiles, de...]
    ppermute x3, starting transfers between devices: 23.1 us -> 0.21 us  [partner(): return lax.ppermute(block, axis, route)]
    ppermute x1, starting transfers between devices: 4.59 us -> 0.47 us  [shards(): from_above = lax.ppermute(picture, 'depth', ring)]
    ppermute x1, starting transfers between devices: 12.3 us -> 8.68 us  [shards(): lax.ppermute(picture[:, row_share - 1:], ('strip', 'depth'), corner)]
    ppermute x3, waiting for transfers between devices: 12 us -> 14.8 us  [partner(): return lax.ppermute(block, axis, route)]
    unnamed x18 -> x16, local copies, waits for them, and re-layouts: 0.81 us -> 2.63 us
  transfers between devices with their start and end apart: 9 -> 9, of which waited for: 4 -> 4; matrix products, arithmetic and copies ran while one was open for 6% -> 4% of each run, Pallas kernels for 0% -> 0%
where the time goes in v3:
time: 99.6 us; the launch traced here: 99.3 us
  Pallas kernels  48.2 us (48%)
  waiting for transfers between devices  21.8 us (22%)
  starting transfers between devices  16.1 us (16%)
  local copies, waits for them, and re-layouts  6.84 us (7%)
  other arithmetic  4 us (4%)
  between operations  2.34 us (2%)
    pallas_call x1, Pallas kernels, march(): pl.pallas_call(functools.partial(march_kernel, optical, layers, tiles, de...  48.2 us
    ppermute x3, waiting for transfers between devices, partner(): return lax.ppermute(block, axis, route)  14.8 us
    ppermute x1, starting transfers between devices, shards(): lax.ppermute(picture[:, row_share - 1:], ('strip', 'depth'), corner)  8.68 us
    ppermute x1, waiting for transfers between devices, shards(): strip_below = lax.ppermute(picture[:, :1], ('strip', 'depth'), corner_back)  6.78 us
    ppermute x1, starting transfers between devices, shards(): above = lax.ppermute(volume[:, rows_here - 1:], 'strip', down_route)  3.12 us
    unnamed x16, local copies, waits for them, and re-layouts  2.63 us
    ppermute x1, starting transfers between devices, shards(): below = lax.ppermute(volume[:, :1], 'strip', up_route)  2.16 us
  transfers between devices with their start and end apart: 9, of which 4 were waited for; matrix products, arithmetic and copies ran while one was open for 4% of the time, Pallas kernels for 0%

profile of v3, /device:TPU:27, one launch (start us, length us, event | category | flops | bytes accessed | tf_op | source)
XLA Modules:
  0.0 99.3 jit_solution(14781805628011599659)
XLA Ops:
  0.0 1.2 %fusion.8 = (bf16[8,1,2048]{2,1,0:T(2,128)(2,1)S(1)}, bf16[8,1,2048]{2,1,0:T(2,128)(2,1)S(1)}) fusion(bf16[8,32,2048]{2,1,0:T(8,128)(2,1)} %vol_ref.1), kind=kLoop, calls=%fused_computation.76 | loop fusion | bytes 131072 | tf_op jit(solution)/shard_map/slice | solution.py:174
  1.2 3.1 %collective-permute-start = (bf16[8,1,2048]{2,1,0:T(2,128)(2,1)S(1)}, bf16[8,1,2048]{2,1,0:T(2,128)(2,1)S(1)}, u32[]{:S(2)}, u32[]{:S(2)}) collective-permute-start(bf16[8,1,2048]{2,1,0:T(2,128)(2,1)S(1)} %get-tuple-element.19), channel_id=1, source_target_pairs={{0,8},{8,16},{16,24},{1,9},{9,17},{17,25},{2,10},{10,18},{18,26},{... | collective-permute-start | bytes 98312 | tf_op jit(solution)/shard_map/ppermute | solution.py:173
  4.4 2.2 %collective-permute-start.1 = (bf16[8,1,2048]{2,1,0:T(2,128)(2,1)S(1)}, bf16[8,1,2048]{2,1,0:T(2,128)(2,1)S(1)}, u32[]{:S(2)}, u32[]{:S(2)}) collective-permute-start(bf16[8,1,2048]{2,1,0:T(2,128)(2,1)S(1)} %get-tuple-element.18), channel_id=1, source_target_pairs={{8,0},{16,8},{24,16},{9,1},{17,9},{25,17},{10,2},{18,10},{26,18},{... | collective-permute-start | bytes 98312 | tf_op jit(solution)/shard_map/ppermute | solution.py:174
  6.5 0.7 reduce-precision_bitcast_fusion.1
  7.3 0.7 multiply_bitcast_fusion.1
  8.2 0.1 mul.227
  8.3 0.7 multiply_bitcast_fusion
  9.2 0.6 copy-done.6
  10.0 0.2 collective-permute-done.1.below_ref
  10.4 0.7 copy-done.1
  11.0 48.2 %march.1 = f32[4,4,8,2048]{3,2,1,0:T(8,128)S(1)} custom-call(s32[16]{0:T(128)S(1)} %bitcast.119, bf16[8,32,2048]{2,1,0:T(8,128)(2,1)S(1)} %copy-done, bf16[8,1,2048]{2,1,0:T(2,128)(2,1)S(1)} %collective-permute-done.above_ref, bf16[8,1,2048]{2,1,0:T(2,128)(2,1)S(1)} %collective-permute-done.1.below_ref, f32[64,144]{1,0:T(8,128)S(1)} %select_maximum_fusion.pattern_ref, ...), custom_call_target="tpu_custom_call" | custom-call | tf_op jit(solution)/shard_map/march/pallas_call | solution.py:144
  59.3 0.6 copy-done.7
  60.0 0.6 dynamic_slice.3
  62.2 6.7 %collective-permute-done.3 = f32[4,1,8,2048]{3,2,0,1:T(8,128)S(1)} collective-permute-done((f32[4,1,8,2048]{3,2,0,1:T(8,128)S(1)}, f32[4,1,8,2048]{3,2,0,1:T(8,128)S(1)}, u32[]{:S(2)}, u32[]{:S(2)}) %collective-permute-start.3) | collective-permute-done | bytes 262176 | tf_op jit(solution)/shard_map/ppermute | solution.py:18
  70.0 0.3 slice_reduce_fusion.8
  70.3 8.1 %collective-permute-done.4 = f32[4,1,4,2048]{3,2,0,1:T(4,128)S(1)} collective-permute-done((f32[4,1,4,2048]{3,2,0,1:T(4,128)S(1)}, f32[4,1,4,2048]{3,2,0,1:T(4,128)S(1)}, u32[]{:S(2)}, u32[]{:S(2)}) %collective-permute-start.4) | collective-permute-done | bytes 131104 | tf_op jit(solution)/shard_map/ppermute | solution.py:18
  78.5 0.5 collective-permute-start.6
  79.0 0.2 pad_slice_fusion.3
  79.2 0.2 collective-permute-start.7
  79.4 8.7 %collective-permute-start.5 = (f32[3,1,2048]{2,1,0:T(1,128)S(1)}, f32[3,1,2048]{2,1,0:T(1,128)S(1)}, u32[]{:S(2)}, u32[]{:S(2)}) collective-permute-start(f32[3,1,2048]{2,1,0:T(1,128)S(1)} %get-tuple-element.28), channel_id=1, source_target_pairs={{7,8},{15,16},{23,24}} | collective-permute-start | bytes 73736 | tf_op jit(solution)/shard_map/ppermute | solution.py:207
  88.0 1.3 %collective-permute-start.8 = (f32[3,1,2048]{2,1,0:T(1,128)S(1)}, f32[3,1,2048]{2,1,0:T(1,128)S(1)}, u32[]{:S(2)}, u32[]{:S(2)}) collective-permute-start(f32[3,1,2048]{2,1,0:T(1,128)S(1)} %get-tuple-element.29), channel_id=1, source_target_pairs={{8,7},{16,15},{24,23}} | collective-permute-start | bytes 73736 | tf_op jit(solution)/shard_map/ppermute | solution.py:208
  89.3 0.2 multiply_reduce_fusion.3
  89.6 0.1 multiply_reduce_fusion.5
  89.8 0.2 pad_slice_fusion.5
  90.0 6.8 %collective-permute-done.8 = f32[3,1,2048]{2,1,0:T(1,128)S(1)} collective-permute-done((f32[3,1,2048]{2,1,0:T(1,128)S(1)}, f32[3,1,2048]{2,1,0:T(1,128)S(1)}, u32[]{:S(2)}, u32[]{:S(2)}) %collective-permute-start.8) | collective-permute-done | bytes 24608 | tf_op jit(solution)/shard_map/ppermute | solution.py:208
  96.9 0.2 pad_slice_fusion.1
  97.0 0.1 multiply_reduce_fusion.1
  97.3 0.2 multiply_reduce_fusion.6
  97.5 0.2 multiply_reduce_fusion
  97.8 0.6 copy-done.4
  98.4 0.2 bitcast_add_fusion
  98.6 0.7 copy.54
  (53 shorter events, 1.9 us)
Async XLA Ops:
  0.0 8.3 %copy-start.5 = (f32[4]{0:T(128)S(1)}, f32[4]{0:T(128)}, u32[]{:S(2)}) copy-start(f32[4]{0:T(128)} %constant.36.clone) | copy-start | bytes 52
  0.0 8.1 %copy-start.3 = (f32[2,8,4]{2,1,0:T(8,128)S(1)}, f32[2,8,4]{2,1,0:T(8,128)}, u32[]{:S(2)}) copy-start(f32[2,8,4]{2,1,0:T(8,128)} %constant.37.clone) | copy-start | bytes 772
  0.0 10.3 %copy-start = (bf16[8,32,2048]{2,1,0:T(8,128)(2,1)S(1)}, bf16[8,32,2048]{2,1,0:T(8,128)(2,1)}, u32[]{:S(2)}) copy-start(bf16[8,32,2048]{2,1,0:T(8,128)(2,1)} %vol_ref.1) | copy-start | bytes 3145732
  1.2 8.8 %collective-permute-start = (bf16[8,1,2048]{2,1,0:T(2,128)(2,1)S(1)}, bf16[8,1,2048]{2,1,0:T(2,128)(2,1)S(1)}, u32[]{:S(2)}, u32[]{:S(2)}) collective-permute-start(bf16[8,1,2048]{2,1,0:T(2,128)(2,1)S(1)} %get-tuple-element.19), channel_id=1, source_target_pairs={{0,8},{8,16},{16,24},{1,9},{9,17},{17,25},{2,10},{10,18},{18,26},{... | collective-permute-start | bytes 98312 | tf_op jit(solution)/shard_map/ppermute | solution.py:173
  4.4 5.9 %collective-permute-start.1 = (bf16[8,1,2048]{2,1,0:T(2,128)(2,1)S(1)}, bf16[8,1,2048]{2,1,0:T(2,128)(2,1)S(1)}, u32[]{:S(2)}, u32[]{:S(2)}) collective-permute-start(bf16[8,1,2048]{2,1,0:T(2,128)(2,1)S(1)} %get-tuple-element.18), channel_id=1, source_target_pairs={{8,0},{16,8},{24,16},{9,1},{17,9},{25,17},{10,2},{18,10},{26,18},{... | collective-permute-start | bytes 98312 | tf_op jit(solution)/shard_map/ppermute | solution.py:174
  9.2 0.7 copy-start.6
  10.3 0.7 copy-start.1
  59.2 2.0 %collective-permute-start.2 = (f32[4,2,8,2048]{3,2,0,1:T(8,128)S(1)}, f32[4,2,8,2048]{3,2,0,1:T(8,128)S(1)}, u32[]{:S(2)}, u32[]{:S(2)}) collective-permute-start(f32[4,2,8,2048]{3,2,0,1:T(8,128)S(1)} %select_bitcast_fusion), channel_id=1, source_target_pairs={{0,1},{1,0},{2,3},{3,2},{4,5},{5,4},{6,7},{7,6},{8,9},{9,8},{10,11... | collective-permute-start | bytes 1572872 | tf_op jit(solution)/shard_map/ppermute | solution.py:18
  59.3 0.7 copy-start.7
  61.5 7.4 %collective-permute-start.3 = (f32[4,1,8,2048]{3,2,0,1:T(8,128)S(1)}, f32[4,1,8,2048]{3,2,0,1:T(8,128)S(1)}, u32[]{:S(2)}, u32[]{:S(2)}) collective-permute-start(f32[4,1,8,2048]{3,2,0,1:T(8,128)S(1)} %select_bitcast_fusion.1), channel_id=1, source_target_pairs={{0,2},{2,0},{1,3},{3,1},{4,6},{6,4},{5,7},{7,5},{8,10},{10,8},{9,1... | collective-permute-start | bytes 786440 | tf_op jit(solution)/shard_map/ppermute | solution.py:18
  69.2 0.8 copy-start.2
  69.2 9.2 %collective-permute-start.4 = (f32[4,1,4,2048]{3,2,0,1:T(4,128)S(1)}, f32[4,1,4,2048]{3,2,0,1:T(4,128)S(1)}, u32[]{:S(2)}, u32[]{:S(2)}) collective-permute-start(f32[4,1,4,2048]{3,2,0,1:T(4,128)S(1)} %select_bitcast_fusion.2), channel_id=1, source_target_pairs={{0,4},{4,0},{1,5},{5,1},{2,6},{6,2},{3,7},{7,3},{8,12},{12,8},{9,1... | collective-permute-start | bytes 393224 | tf_op jit(solution)/shard_map/ppermute | solution.py:18
  78.5 11.2 %collective-permute-start.6 = (f32[3,4,2048]{2,1,0:T(4,128)S(1)}, f32[3,4,2048]{2,1,0:T(4,128)S(1)}, u32[]{:S(2)}, u32[]{:S(2)}) collective-permute-start(f32[3,4,2048]{2,1,0:T(4,128)S(1)} %fusion.5), channel_id=1, source_target_pairs={{0,1},{1,2},{2,3},{3,4},{4,5},{5,6},{6,7},{7,0},{8,9},{9,10},{10,1... | collective-permute-start | bytes 294920 | tf_op jit(solution)/shard_map/ppermute | solution.py:205
  79.2 10.8 %collective-permute-start.7 = (f32[3,4,2048]{2,1,0:T(4,128)S(1)}, f32[3,4,2048]{2,1,0:T(4,128)S(1)}, u32[]{:S(2)}, u32[]{:S(2)}) collective-permute-start(f32[3,4,2048]{2,1,0:T(4,128)S(1)} %fusion.5), channel_id=1, source_target_pairs={{1,0},{2,1},{3,2},{4,3},{5,4},{6,5},{7,6},{0,7},{9,8},{10,9},{11,1... | collective-permute-start | bytes 294920 | tf_op jit(solution)/shard_map/ppermute | solution.py:206
  79.4 10.3 %collective-permute-start.5 = (f32[3,1,2048]{2,1,0:T(1,128)S(1)}, f32[3,1,2048]{2,1,0:T(1,128)S(1)}, u32[]{:S(2)}, u32[]{:S(2)}) collective-permute-start(f32[3,1,2048]{2,1,0:T(1,128)S(1)} %get-tuple-element.28), channel_id=1, source_target_pairs={{7,8},{15,16},{23,24}} | collective-permute-start | bytes 73736 | tf_op jit(solution)/shard_map/ppermute | solution.py:207
  88.0 8.7 %collective-permute-start.8 = (f32[3,1,2048]{2,1,0:T(1,128)S(1)}, f32[3,1,2048]{2,1,0:T(1,128)S(1)}, u32[]{:S(2)}, u32[]{:S(2)}) collective-permute-start(f32[3,1,2048]{2,1,0:T(1,128)S(1)} %get-tuple-element.29), channel_id=1, source_target_pairs={{8,7},{16,15},{24,23}} | collective-permute-start | bytes 73736 | tf_op jit(solution)/shard_map/ppermute | solution.py:208
  97.7 0.7 copy-start.4
